TPU v7x, 128 devices: a whole 4x4x4 slice. The times are simulated.
128 devices in a mesh: row: 16 (over z, x), mp: 8 (over y, core).
Axes of the slice: x: 4, y: 4, z: 4, core: 2. Of those that a mesh axis runs over, the one named last changes fastest.
Arguments:
- token_ids: int32 [128, 128], P('row'), may hold values from 0 to 511
- set_lengths: int32 [128], P('row'), may hold values from 32 to 128
- live_counts: int32 [16], replicated, may hold values from 1 to 8, 64 in all
- embed_table: bfloat16 [512, 5120], replicated, may hold values from -3 to 3
- position_table: bfloat16 [128, 5120], replicated, may hold values from -3 to 3
- norm_gain: float32 [5120], replicated, may hold values from 0.1 to 1.9
- w_query: bfloat16 [5120, 5120], P('row', 'mp')
- w_key: bfloat16 [5120, 5120], P('row', 'mp')
- w_value: bfloat16 [5120, 5120], P('row', 'mp'), may hold values from -0.078125 to 0.078125
- w_out: bfloat16 [5120, 5120], P('mp', 'row'), may hold values from -0.078125 to 0.078125
Outputs:
- verified: bfloat16 [128, 128, 5120], P('row', None, 'mp')
Inputs may be any that keep to these rules, and one draw needn't show every extreme that they name: Owner group g has live_counts[g] live sets, its first slots; the counts sum to 64 and one group holds 8. `set_lengths`: positions at or past a set's length are padding.
All inputs are finite; a program needn't handle non-finite values.
Results may differ from a plain program's by a relative error of at most 0.017.
Values may be sent and summed in bfloat16 or wider, within the bound.
No kernel may reach another device: no remote copies, remote signals or barrier semaphores. Data moves between devices by JAX's collectives and lax.ppermute only.
A program may use at most 128 MiB of HBM per device.

v0:
```python
import jax
import jax.numpy as jnp
from jax import lax
from jax.experimental import pallas as pl
from jax.experimental.pallas import tpu as pltpu
from jax.sharding import PartitionSpec as P

D = 5120
DH = 128
HEADS = 5
ROWS = 16
VOCAB = 512
SEQ = 128
SLOTS = 8
TABLE = VOCAB + SEQ
BLOCK = D // ROWS
FEATURES = 640
HALF = DH // 2
SIDE = 4
F32 = jnp.float32
BF16 = jnp.bfloat16
VMEM = 16 << 20
NOTE = 16
GROUP = 16
CAPACITIES = (640, 704, 768, 832, 896, SLOTS * SEQ)


def mm(a, b, dims):
    return lax.dot_general(a, b, (dims, ((), ())), preferred_element_type=F32)


def pack_kernel(place_ref, lens_ref, counts_ref, gain_ref, q_hbm, k_hbm, v_hbm, out_ref, info_ref, w_ref, turned_ref, sems):
    row = place_ref[0]
    copies = [
        pltpu.make_async_copy(source, w_ref.at[j], sems.at[j])
        for j, source in enumerate((q_hbm, k_hbm, v_hbm))
    ]
    for copy in copies:
        copy.start()
    live = counts_ref[row]
    total = jnp.int32(0)
    for s in range(SLOTS):
        info_ref[s] = GROUP * total
        groups = (lens_ref[s] + GROUP - 1) // GROUP
        total = total + jnp.where(s < live, groups, 0)
    info_ref[SLOTS] = live
    line = jnp.broadcast_to(gain_ref[pl.ds(row // 2, 1), :], (8, 2 * BLOCK))
    turned_ref[...] = line.T
    start = pl.multiple_of((row % 2) * BLOCK, 8)
    gain = turned_ref[pl.ds(start, BLOCK), :][:, :1]
    out_ref[ROWS - 1, :BLOCK] = jnp.zeros((BLOCK, DH), BF16)
    count = jnp.full((NOTE, DH), total, jnp.int32).astype(F32).astype(BF16)
    for i in range(ROWS):
        out_ref[i, BLOCK:] = count
    for j, copy in enumerate(copies):
        copy.wait()
        for h in range(HEADS):
            block = gain * w_ref[j, :, DH * h : DH * (h + 1)].astype(F32)
            out_ref[HEADS * j + h, :BLOCK] = block.astype(BF16)


def pack(place, lengths, counts, gain, w_query, w_key, w_value):
    stay = pl.BlockSpec(memory_space=pltpu.HBM)
    return pl.pallas_call(
        pack_kernel,
        grid_spec=pltpu.PrefetchScalarGridSpec(
            num_scalar_prefetch=3,
            grid=(1,),
            in_specs=[pl.BlockSpec((8, 2 * BLOCK), lambda i, *_: (0, 0)), stay, stay, stay],
            out_specs=[
                pl.BlockSpec((ROWS, BLOCK + NOTE, DH), lambda i, *_: (0, 0, 0)),
                pl.BlockSpec(memory_space=pltpu.SMEM),
            ],
            scratch_shapes=[
                pltpu.VMEM((3, BLOCK, FEATURES), BF16),
                pltpu.VMEM((2 * BLOCK, 8), F32),
                pltpu.SemaphoreType.DMA((3,)),
            ],
        ),
        out_shape=[
            jax.ShapeDtypeStruct((ROWS, BLOCK + NOTE, DH), BF16),
            jax.ShapeDtypeStruct((2 * SLOTS,), jnp.int32),
        ],
        compiler_params=pltpu.CompilerParams(vmem_limit_bytes=VMEM),
        name="pack",
    )(place, lengths, counts, gain, w_query, w_key, w_value)


def table_kernel(e_ref, p_ref, w_ref, t_ref, t_acc):
    step = pl.program_id(0)

    @pl.when(step == 0)
    def _():
        t_acc[...] = jnp.zeros_like(t_acc)

    w = w_ref[:, :BLOCK].reshape(2 * BLOCK, DH)
    t_acc[:, :VOCAB] += mm(w, e_ref[...], ((0,), (1,)))
    t_acc[:, VOCAB:] += mm(w, p_ref[...], ((0,), (1,)))

    @pl.when(step == pl.num_programs(0) - 1)
    def _():
        t_ref[...] = t_acc[...].astype(BF16)


def project_tables(embed_table, position_table, w_block):
    return pl.pallas_call(
        table_kernel,
        grid=(ROWS // 2,),
        in_specs=[
            pl.BlockSpec((VOCAB, 2 * BLOCK), lambda k: (0, k)),
            pl.BlockSpec((SEQ, 2 * BLOCK), lambda k: (0, k)),
            pl.BlockSpec((2, BLOCK + NOTE, DH), lambda k: (k, 0, 0)),
        ],
        out_specs=pl.BlockSpec((DH, TABLE), lambda k: (0, 0)),
        out_shape=jax.ShapeDtypeStruct((DH, TABLE), BF16),
        scratch_shapes=[pltpu.VMEM((DH, TABLE), F32)],
        compiler_params=pltpu.CompilerParams(vmem_limit_bytes=VMEM),
        name="project_tables",
    )(embed_table, position_table, w_block)


def scale_kernel(e_ref, p_ref, r_ref, g_acc, ee_acc, pp_acc):
    step = pl.program_id(0)

    @pl.when(step == 0)
    def _():
        g_acc[...] = jnp.zeros_like(g_acc)
        ee_acc[...] = jnp.zeros_like(ee_acc)
        pp_acc[...] = jnp.zeros_like(pp_acc)

    e, p = e_ref[...], p_ref[...]
    g_acc[...] += mm(e, p, ((1,), (1,)))
    pp_acc[...] += mm(p, p, ((1,), (1,)))
    wide = e.astype(F32)
    square = wide * wide
    folded = square[:, :128]
    for k in range(1, 2 * BLOCK // 128):
        folded += square[:, 128 * k : 128 * (k + 1)]
    ee_acc[...] += folded

    @pl.when(step == pl.num_programs(0) - 1)
    def _():
        ee = jnp.sum(ee_acc[...], axis=1, keepdims=True)
        diagonal = lax.broadcasted_iota(jnp.int32, (SEQ, SEQ), 0) == lax.broadcasted_iota(
            jnp.int32, (SEQ, SEQ), 1
        )
        pp = jnp.sum(jnp.where(diagonal, pp_acc[...], 0.0), axis=0, keepdims=True)
        total = jnp.maximum(ee + 2.0 * g_acc[...] + pp, 0.0)
        r_ref[...] = lax.rsqrt(total * (1.0 / D) + 1e-05)


def norm_scales(embed_table, position_table):
    return pl.pallas_call(
        scale_kernel,
        grid=(ROWS // 2,),
        in_specs=[
            pl.BlockSpec((VOCAB, 2 * BLOCK), lambda k: (0, k)),
            pl.BlockSpec((SEQ, 2 * BLOCK), lambda k: (0, k)),
        ],
        out_specs=pl.BlockSpec((VOCAB, SEQ), lambda k: (0, 0)),
        out_shape=jax.ShapeDtypeStruct((VOCAB, SEQ), F32),
        scratch_shapes=[
            pltpu.VMEM((VOCAB, SEQ), F32),
            pltpu.VMEM((VOCAB, 128), F32),
            pltpu.VMEM((SEQ, SEQ), F32),
        ],
        compiler_params=pltpu.CompilerParams(vmem_limit_bytes=VMEM),
        cost_estimate=pl.CostEstimate(flops=2 * TABLE * SEQ * D, transcendentals=VOCAB * SEQ, bytes_accessed=2 * TABLE * D),
        name="norm_scales",
    )(embed_table, position_table)


def residual_kernel(info_ref, place_ref, ids_ref, e_ref, p_ref, out_ref):
    slot = pl.program_id(0)

    @pl.when(slot < info_ref[SLOTS])
    def _():
        hit = lax.broadcasted_iota(jnp.int32, (VOCAB, SEQ), 0) == ids_ref[pl.ds(slot, 1), :]
        pick = jnp.where(hit, 1.0, 0.0).astype(BF16)
        stored = mm(pick, e_ref[...], ((0,), (0,))) + p_ref[...].astype(F32)
        out_ref[0] = stored.astype(BF16)

    @pl.when(slot >= info_ref[SLOTS])
    def _():
        out_ref[...] = jnp.zeros_like(out_ref)


def residual(info, place, ids, embed_table, position_table):
    return pl.pallas_call(
        residual_kernel,
        grid_spec=pltpu.PrefetchScalarGridSpec(
            num_scalar_prefetch=2,
            grid=(SLOTS,),
            in_specs=[
                pl.BlockSpec((SLOTS, SEQ), lambda s, *_: (0, 0)),
                pl.BlockSpec((VOCAB, FEATURES), lambda s, info, place: (0, place[1])),
                pl.BlockSpec((SEQ, FEATURES), lambda s, info, place: (0, place[1])),
            ],
            out_specs=pl.BlockSpec((1, SEQ, FEATURES), lambda s, *_: (s, 0, 0)),
        ),
        out_shape=jax.ShapeDtypeStruct((SLOTS, SEQ, FEATURES), BF16),
        compiler_params=pltpu.CompilerParams(vmem_limit_bytes=VMEM),
        cost_estimate=pl.CostEstimate(flops=2 * SLOTS * SEQ * VOCAB * FEATURES, transcendentals=0, bytes_accessed=4 * SLOTS * SEQ * FEATURES),
        name="residual",
    )(info, place, ids, embed_table, position_table)


def attend_kernel(lens_ref, info_ref, place_ref, ids_ref, r_ref, *refs):
    a_refs, b_refs = refs[:SIDE], refs[SIDE : 2 * SIDE]
    out_ref, table_ref, set_ref = refs[2 * SIDE :]
    step = pl.program_id(0)
    z, x = place_ref[0] // SIDE, place_ref[0] % SIDE

    @pl.when(step == 0)
    def _():
        for dz in range(SIDE):
            for dx in range(SIDE):
                source = SIDE * ((z + SIDE - dz) % SIDE) + (x + SIDE - dx) % SIDE
                table_ref[pl.ds(source, 1), :HALF] = a_refs[dz][dx : dx + 1]
                table_ref[pl.ds(source, 1), HALF:] = b_refs[dx][dz : dz + 1]
        out_ref[...] = jnp.zeros_like(out_ref)

    @pl.when(2 * step < info_ref[SLOTS])
    def _():
        vocab = lax.broadcasted_iota(jnp.int32, (VOCAB, SEQ), 0)
        eye = lax.broadcasted_iota(jnp.int32, (SEQ, SEQ), 0) == lax.broadcasted_iota(
            jnp.int32, (SEQ, SEQ), 1
        )
        picks, scales = [], []
        for s in range(2):
            hit = vocab == ids_ref[pl.ds(2 * step + s, 1), :]
            scales.append(jnp.sum(jnp.where(hit, r_ref[...], 0.0), axis=0, keepdims=True))
            picks.append(
                jnp.concatenate(
                    [jnp.where(hit, 1.0, 0.0).astype(BF16), jnp.where(eye, 1.0, 0.0).astype(BF16)], 0
                )
            )
        pick = jnp.concatenate(picks, axis=1)
        scale = jnp.concatenate(scales, axis=1)
        table = table_ref[: 3 * HEADS].reshape(3 * HEADS * DH, TABLE)
        rows = (mm(table, pick, ((1,), (0,))) * scale).astype(BF16)
        key_at = lax.broadcasted_iota(jnp.int32, (SEQ, SEQ), 0)
        for s in range(2):
            valid = key_at < lens_ref[2 * step + s]
            cols = slice(SEQ * s, SEQ * (s + 1))
            for h in range(HEADS):
                q = rows[DH * h : DH * (h + 1), cols]
                k = rows[DH * (HEADS + h) : DH * (HEADS + h + 1), cols]
                v = rows[DH * (2 * HEADS + h) : DH * (2 * HEADS + h + 1), cols]
                scores = mm(k, q, ((0,), (0,))) * DH ** (-0.5)
                scores = jnp.where(valid, scores, -1e30)
                expo = jnp.exp(scores - jnp.max(scores, axis=0, keepdims=True))
                weights = (expo / jnp.sum(expo, axis=0, keepdims=True)).astype(BF16)
                mixed = mm(v, weights, ((1,), (0,)))
                set_ref[s, :, DH * h : DH * (h + 1)] = mixed.T.astype(BF16)
        for s in range(2):
            for i in range(SEQ // GROUP):

                @pl.when((2 * step + s < info_ref[SLOTS]) & (GROUP * i < lens_ref[2 * step + s]))
                def _(s=s, i=i):
                    at = pl.multiple_of(info_ref[2 * step + s] + GROUP * i, GROUP)
                    out_ref[pl.ds(at, GROUP), :] = set_ref[s, GROUP * i : GROUP * (i + 1), :]


def attend(capacity, lengths, info, place, ids, r, a_parts, b_parts):
    quarter = pl.BlockSpec((SIDE, HALF, TABLE), lambda i, *_: (0, 0, 0))
    return pl.pallas_call(
        attend_kernel,
        grid_spec=pltpu.PrefetchScalarGridSpec(
            num_scalar_prefetch=3,
            grid=(SLOTS // 2,),
            in_specs=[
                pl.BlockSpec((SLOTS, SEQ), lambda i, *_: (0, 0)),
                pl.BlockSpec((VOCAB, SEQ), lambda i, *_: (0, 0)),
                *[quarter] * (2 * SIDE),
            ],
            out_specs=pl.BlockSpec((capacity, FEATURES), lambda i, *_: (0, 0)),
            scratch_shapes=[
                pltpu.VMEM((ROWS, DH, TABLE), BF16),
                pltpu.VMEM((2, SEQ, FEATURES), BF16),
            ],
        ),
        out_shape=jax.ShapeDtypeStruct((capacity, FEATURES), BF16),
        compiler_params=pltpu.CompilerParams(vmem_limit_bytes=VMEM),
        name="attend",
    )(lengths, info, place, ids, r, *a_parts, *b_parts)


def product(a_ref, other_ref, w_ref, w_other_ref):
    mine = mm(a_ref[...], w_ref[...].reshape(FEATURES, FEATURES), ((1,), (1,)))
    theirs = jnp.concatenate([w_other_ref[1], w_other_ref[0]], axis=0)
    return mine + mm(other_ref[...], theirs, ((1,), (1,)))


def pick(ahead):
    def block(place, core):
        return 2 * ((place[3] + ahead) % SIDE) + core

    shape = (2, BLOCK, FEATURES)
    return [
        pl.BlockSpec(shape, lambda i, place: (block(place, place[2]), 0, 0)),
        pl.BlockSpec(shape, lambda i, place: (block(place, 1 - place[2]), 0, 0)),
    ]


def far_kernel(place_ref, a_ref, other_ref, w_ref, w_other_ref, top_ref, bottom_ref):
    half = pl.program_id(0)
    total = product(a_ref, other_ref, w_ref, w_other_ref).astype(BF16)

    @pl.when(half == 0)
    def _():
        top_ref[...] = total

    @pl.when(half == 1)
    def _():
        bottom_ref[...] = total


def far_partials(place, mixed, other, w):
    tile = mixed.shape[0] // 2
    rows = pl.BlockSpec((tile, FEATURES), lambda i, place: (i, 0))
    whole = pl.BlockSpec((tile, FEATURES), lambda i, place: (0, 0))
    return pl.pallas_call(
        far_kernel,
        grid_spec=pltpu.PrefetchScalarGridSpec(
            num_scalar_prefetch=1,
            grid=(2,),
            in_specs=[rows, rows, *pick(2)],
            out_specs=[whole, whole],
        ),
        out_shape=[jax.ShapeDtypeStruct((tile, FEATURES), BF16)] * 2,
        compiler_params=pltpu.CompilerParams(vmem_limit_bytes=VMEM),
        name="far_partials",
    )(place, mixed, other, w, w)


def free_kernel(place_ref, a0, o0, a1, o1, w0, w1, w2, w3, up_ref, down_ref):
    up_ref[...] = product(a1, o1, w0, w1).astype(BF16)
    down_ref[...] = product(a0, o0, w2, w3).astype(BF16)


def free_partials(place, mixed, other, w):
    tile = mixed.shape[0] // 2
    first = pl.BlockSpec((tile, FEATURES), lambda i, place: (0, 0))
    second = pl.BlockSpec((tile, FEATURES), lambda i, place: (1, 0))
    return pl.pallas_call(
        free_kernel,
        grid_spec=pltpu.PrefetchScalarGridSpec(
            num_scalar_prefetch=1,
            grid=(1,),
            in_specs=[first, first, second, second, *pick(1), *pick(3)],
            out_specs=[first, first],
        ),
        out_shape=[jax.ShapeDtypeStruct((tile, FEATURES), BF16)] * 2,
        compiler_params=pltpu.CompilerParams(vmem_limit_bytes=VMEM),
        name="free_partials",
    )(place, mixed, other, mixed, other, w, w, w, w)


def relay_kernel(place_ref, a0, o0, a1, o1, w0, w1, w2, w3, from_below, from_above, up_ref, down_ref):
    up_ref[...] = (product(a0, o0, w0, w1) + from_below[...].astype(F32)).astype(BF16)
    down_ref[...] = (product(a1, o1, w2, w3) + from_above[...].astype(F32)).astype(BF16)


def relay_partials(place, mixed, other, w, from_below, from_above):
    tile = mixed.shape[0] // 2
    first = pl.BlockSpec((tile, FEATURES), lambda i, place: (0, 0))
    second = pl.BlockSpec((tile, FEATURES), lambda i, place: (1, 0))
    return pl.pallas_call(
        relay_kernel,
        grid_spec=pltpu.PrefetchScalarGridSpec(
            num_scalar_prefetch=1,
            grid=(1,),
            in_specs=[first, first, second, second, *pick(1), *pick(3), first, first],
            out_specs=[first, first],
        ),
        out_shape=[jax.ShapeDtypeStruct((tile, FEATURES), BF16)] * 2,
        compiler_params=pltpu.CompilerParams(vmem_limit_bytes=VMEM),
        name="relay_partials",
    )(place, mixed, other, mixed, other, w, w, w, w, from_below, from_above)


def base_kernel(place_ref, a_ref, other_ref, w_ref, w_other_ref, out_ref):
    out_ref[...] = product(a_ref, other_ref, w_ref, w_other_ref)


def base_partial(place, mixed, other, w):
    tokens = mixed.shape[0]
    rows = pl.BlockSpec((tokens // 2, FEATURES), lambda i, place: (i, 0))
    return pl.pallas_call(
        base_kernel,
        grid_spec=pltpu.PrefetchScalarGridSpec(
            num_scalar_prefetch=1,
            grid=(2,),
            in_specs=[rows, rows, *pick(0)],
            out_specs=rows,
        ),
        out_shape=jax.ShapeDtypeStruct((tokens, FEATURES), F32),
        compiler_params=pltpu.CompilerParams(vmem_limit_bytes=VMEM),
        name="base_partial",
    )(place, mixed, other, w, w)


def finish_kernel(lens_ref, info_ref, stored_ref, base_ref, *refs):
    below, above, out_ref = refs[:2], refs[2:4], refs[4]
    slot = pl.program_id(0)
    tile = below[0].shape[0]
    for i in range(SEQ // GROUP):
        here = slice(GROUP * i, GROUP * (i + 1))
        live = (slot < info_ref[SLOTS]) & (GROUP * i < lens_ref[slot])
        start = pl.multiple_of(info_ref[slot] + GROUP * i, GROUP)
        for half in range(2):

            @pl.when(live & ((start >= tile) if half else (start < tile)))
            def _(i=i, here=here, half=half, start=start):
                at = pl.ds(pl.multiple_of(start - half * tile, GROUP), GROUP)
                total = base_ref[pl.ds(start, GROUP), :] + below[half][at, :].astype(F32)
                total += above[half][at, :].astype(F32)
                place = GROUP * i + lax.broadcasted_iota(jnp.int32, (GROUP, FEATURES), 0)
                result = stored_ref[0, here].astype(F32) + total
                out_ref[0, here] = jnp.where(place < lens_ref[slot], result, 0.0).astype(BF16)

        @pl.when(jnp.logical_not(live))
        def _(here=here):
            out_ref[0, here] = jnp.zeros((GROUP, FEATURES), BF16)


def finish(lengths, info, stored, base, below, above):
    whole = pl.BlockSpec(base.shape, lambda s, *_: (0, 0))
    half = pl.BlockSpec(below[0].shape, lambda s, *_: (0, 0))
    one = pl.BlockSpec((1, SEQ, FEATURES), lambda s, *_: (s, 0, 0))
    return pl.pallas_call(
        finish_kernel,
        grid_spec=pltpu.PrefetchScalarGridSpec(
            num_scalar_prefetch=2,
            grid=(SLOTS,),
            in_specs=[one, whole, half, half, half, half],
            out_specs=one,
        ),
        out_shape=jax.ShapeDtypeStruct((SLOTS, SEQ, FEATURES), BF16),
        compiler_params=pltpu.CompilerParams(vmem_limit_bytes=VMEM),
        name="finish",
    )(lengths, info, stored, base, *below, *above)


def on_device(
    token_ids,
    set_lengths,
    live_counts,
    embed_table,
    position_table,
    norm_gain,
    w_query,
    w_key,
    w_value,
    w_out,
):
    row = lax.axis_index("row")
    part = lax.axis_index("mp")
    y, core = part // 2, part % 2
    place = jnp.stack([row, part, core, y])

    def shifted(o, along_x):
        pairs = []
        for z in range(SIDE):
            for x in range(SIDE):
                to = SIDE * z + (x + o) % SIDE if along_x else SIDE * ((z + o) % SIDE) + x
                pairs.append((SIDE * z + x, to))
        return pairs

    def spread(value, along_x):
        near = {o: lax.ppermute(value, "row", shifted(o, along_x)) for o in (1, 3, 2)}
        return [value, near[1], near[2], near[3]]

    turned = w_out.T
    cross = []
    for z in range(SIDE):
        for x in range(SIDE):
            for line in range(SIDE):
                c = 1 - x // 2
                source = (SIDE * z + x) * 8 + 2 * line + c
                cross.append((source, (SIDE * z + 3 - x) * 8 + 2 * line + 1 - c))
    crossed = lax.ppermute(turned, ("row", "mp"), cross)
    tiles = jnp.where((row % SIDE) // 2 == core, turned, crossed)

    packed, info = pack(
        place, set_lengths, live_counts, norm_gain.reshape(8, 2 * BLOCK), w_query, w_key, w_value
    )
    w_block = lax.all_to_all(packed, "row", 0, 0)
    w_block, tiles = lax.optimization_barrier((w_block, tiles))
    w_all = lax.all_gather(tiles, "row", axis=0)
    most = GROUP * jnp.max(w_block[:, BLOCK, 0].astype(F32)).astype(jnp.int32)
    mine = project_tables(embed_table, position_table, w_block)

    a_line = jnp.stack(spread(mine[:HALF], True))
    b_line = jnp.stack(spread(mine[HALF:], False))
    a_line, b_line = lax.optimization_barrier((a_line, b_line))
    a_parts, b_parts = spread(a_line, False), spread(b_line, True)
    embed_late, a_parts[1] = lax.optimization_barrier((embed_table, a_parts[1]))
    r = norm_scales(embed_late, position_table)

    swap = [(2 * i + c, 2 * i + 1 - c) for i in range(SIDE) for c in range(2)]

    def along(o):
        return [(2 * i + c, 2 * ((i + o) % SIDE) + c) for i in range(SIDE) for c in range(2)]

    def rest(capacity, a_parts, b_parts, w, r):
        mixed = attend(capacity, set_lengths, info, place, token_ids, r, a_parts, b_parts)
        other = lax.ppermute(mixed, "mp", swap)
        top, bottom = far_partials(place, mixed, other, w)
        from_below = lax.ppermute(top, "mp", along(1))
        from_above = lax.ppermute(bottom, "mp", along(3))
        free_up, free_down = free_partials(place, mixed, other, w)
        below_low = lax.ppermute(free_up, "mp", along(1))
        above_high = lax.ppermute(free_down, "mp", along(3))
        up, down = relay_partials(place, mixed, other, w, from_below, from_above)
        below_high = lax.ppermute(up, "mp", along(1))
        above_low = lax.ppermute(down, "mp", along(3))
        base = base_partial(place, mixed, other, w)
        stored = residual(info, place, token_ids, embed_table, position_table)
        return finish(
            set_lengths, info, stored, base, (below_high, below_low), (above_high, above_low)
        )

    return rest(SLOTS * SEQ, a_parts, b_parts, w_all, r)


def solution(mesh):
    in_specs = (
        P("row", None),
        P("row"),
        P(),
        P(),
        P(),
        P(),
        P("row", "mp"),
        P("row", "mp"),
        P("row", "mp"),
        P("mp", "row"),
    )
    out_specs = P("row", None, "mp")
    return jax.shard_map(
        on_device, mesh=mesh, in_specs=in_specs, out_specs=out_specs, check_vma=False
    )
```

profile of v0, /device:TPU:8, one launch (start us, length us, event | category | flops | bytes accessed | tf_op | source)
XLA Modules:
  0.0 179.6 jit_solution(14879000986518622206)
XLA Ops:
  11.7 2.2 %pack.1 = (bf16[16,336,128]{2,1,0:T(8,128)(2,1)S(1)}, s32[16]{0:T(128)S(1)}) custom-call(s32[4]{0:T(128)S(1)} %pad_add_fusion.place_ref, s32[8]{0:T(128)S(1)} %copy-done.9, s32[16]{0:T(128)S(1)} %copy-done.11, f32[8,640]{1,0:T(8,128)S(1)} %reshape.3.gain_ref, bf16[320,640]{1,0:T(8,128)(2,1)S(1)} %copy-done.5, bf16[320,640]{1,0:T(8,128)(2,1)S(1)} %copy-done.6, ...), custom_call_target="tpu_custom_call" | custom-call | tf_op jit(solution)/shard_map/pack/pallas_call | solution.py:64
  15.1 8.0 %all-to-all-start = ((bf16[16,336,128]{2,1,0:T(8,128)(2,1)}), bf16[16,336,128]{2,1,0:T(8,128)(2,1)S(1)}, u32[]{:S(2)}, u32[]{:S(2)}) async-start(bf16[16,336,128]{2,1,0:T(8,128)(2,1)} %copy-done.4), calls=%async_computation | async-start | bytes 2752512 | tf_op jit(solution)/shard_map/all_to_all | solution.py:489
  24.8 19.7 %all-to-all-done.w_ref = bf16[16,336,128]{2,1,0:T(8,128)(2,1)S(1)} async-done(((bf16[16,336,128]{2,1,0:T(8,128)(2,1)}), bf16[16,336,128]{2,1,0:T(8,128)(2,1)S(1)}, u32[]{:S(2)}, u32[]{:S(2)}) %all-to-all-start) | async-done | bytes 1376288 | tf_op jit(solution)/shard_map/all_to_all | solution.py:489
  44.6 2.5 %copy-done.1 = bf16[512,5120]{1,0:T(8,128)(2,1)S(1)} copy-done((bf16[512,5120]{1,0:T(8,128)(2,1)S(1)}, bf16[512,5120]{1,0:T(8,128)(2,1)}, u32[]{:S(2)}) %copy-start.1) | copy-done | bytes 5242904
  47.0 4.0 %project_tables.1 = bf16[128,640]{1,0:T(8,128)(2,1)S(1)} custom-call(bf16[512,5120]{1,0:T(8,128)(2,1)S(1)} %copy-done.1, bf16[128,5120]{1,0:T(8,128)(2,1)S(1)} %copy-done.2, bf16[16,336,128]{2,1,0:T(8,128)(2,1)S(1)} %all-to-all-done.w_ref), custom_call_target="tpu_custom_call" | custom-call | tf_op jit(solution)/shard_map/project_tables/pallas_call | solution.py:106
  51.2 2.0 %collective-permute-start.5 = (bf16[64,640]{1,0:T(8,128)(2,1)S(1)}, bf16[64,640]{1,0:T(8,128)(2,1)S(1)}, u32[]{:S(2)}, u32[]{:S(2)}) collective-permute-start(bf16[64,640]{1,0:T(8,128)(2,1)S(1)} %get-tuple-element.35), channel_id=1, source_target_pairs={{0,64},{8,72},{16,80},{24,88},{32,96},{40,104},{48,112},{56,120},{... | collective-permute-start | bytes 245768 | tf_op jit(solution)/shard_map/ppermute | solution.py:472
  53.2 1.6 collective-permute-start.6
  54.8 6.3 %collective-permute-start.2 = (bf16[64,640]{1,0:T(8,128)(2,1)S(1)}, bf16[64,640]{1,0:T(8,128)(2,1)S(1)}, u32[]{:S(2)}, u32[]{:S(2)}) collective-permute-start(bf16[64,640]{1,0:T(8,128)(2,1)S(1)} %get-tuple-element.36), channel_id=1, source_target_pairs={{0,16},{8,24},{16,0},{24,8},{32,48},{40,56},{48,32},{56,40},{64,80... | collective-permute-start | bytes 245768 | tf_op jit(solution)/shard_map/ppermute | solution.py:472
  61.1 2.6 %collective-permute-start.3 = (bf16[64,640]{1,0:T(8,128)(2,1)S(1)}, bf16[64,640]{1,0:T(8,128)(2,1)S(1)}, u32[]{:S(2)}, u32[]{:S(2)}) collective-permute-start(bf16[64,640]{1,0:T(8,128)(2,1)S(1)} %get-tuple-element.36), channel_id=1, source_target_pairs={{0,24},{8,0},{16,8},{24,16},{32,56},{40,32},{48,40},{56,48},{64,88... | collective-permute-start | bytes 245768 | tf_op jit(solution)/shard_map/ppermute | solution.py:472
  64.6 2.9 %collective-permute-done.2 = bf16[64,640]{1,0:T(8,128)(2,1)S(1)} collective-permute-done((bf16[64,640]{1,0:T(8,128)(2,1)S(1)}, bf16[64,640]{1,0:T(8,128)(2,1)S(1)}, u32[]{:S(2)}, u32[]{:S(2)}) %collective-permute-start.2) | collective-permute-done | bytes 81952 | tf_op jit(solution)/shard_map/ppermute | solution.py:472
  70.0 2.5 %collective-permute-start.11 = (bf16[4,64,640]{2,1,0:T(8,128)(2,1)S(1)}, bf16[4,64,640]{2,1,0:T(8,128)(2,1)S(1)}, u32[]{:S(2)}, u32[]{:S(2)}) collective-permute-start(bf16[4,64,640]{2,1,0:T(8,128)(2,1)S(1)} %pad_maximum_fusion.1.refs_4_), channel_id=1, source_target_pairs={{0,16},{8,24},{16,0},{24,8},{32,48},{40,56},{48,32},{56,40},{64,80... | collective-permute-start | bytes 983048 | tf_op jit(solution)/shard_map/ppermute | solution.py:472
  72.5 2.6 %collective-permute-start.12 = (bf16[4,64,640]{2,1,0:T(8,128)(2,1)S(1)}, bf16[4,64,640]{2,1,0:T(8,128)(2,1)S(1)}, u32[]{:S(2)}, u32[]{:S(2)}) collective-permute-start(bf16[4,64,640]{2,1,0:T(8,128)(2,1)S(1)} %pad_maximum_fusion.1.refs_4_), channel_id=1, source_target_pairs={{0,24},{8,0},{16,8},{24,16},{32,56},{40,32},{48,40},{56,48},{64,88... | collective-permute-start | bytes 983048 | tf_op jit(solution)/shard_map/ppermute | solution.py:472
  75.1 4.2 %collective-permute-done.7.refs_1_ = bf16[4,64,640]{2,1,0:T(8,128)(2,1)S(1)} collective-permute-done((bf16[4,64,640]{2,1,0:T(8,128)(2,1)S(1)}, bf16[4,64,640]{2,1,0:T(8,128)(2,1)S(1)}, u32[]{:S(2)}, u32[]{:S(2)}) %collective-permute-start.7) | collective-permute-done | bytes 327712 | tf_op jit(solution)/shard_map/ppermute | solution.py:472
  80.5 4.2 %norm_scales.1.r_ref = f32[512,128]{1,0:T(8,128)S(1)} custom-call(bf16[512,5120]{1,0:T(8,128)(2,1)S(1)} %copy-done.1, bf16[128,5120]{1,0:T(8,128)(2,1)S(1)} %copy-done.2), custom_call_target="tpu_custom_call" | custom-call | flops 838860800 | bytes 6553600 | tf_op jit(solution)/shard_map/norm_scales/pallas_call | solution.py:153
  84.7 3.7 %collective-permute-done.10.refs_5_ = bf16[4,64,640]{2,1,0:T(8,128)(2,1)S(1)} collective-permute-done((bf16[4,64,640]{2,1,0:T(8,128)(2,1)S(1)}, bf16[4,64,640]{2,1,0:T(8,128)(2,1)S(1)}, u32[]{:S(2)}, u32[]{:S(2)}) %collective-permute-start.10) | collective-permute-done | bytes 327712 | tf_op jit(solution)/shard_map/ppermute | solution.py:472
  88.4 2.5 %collective-permute-done.12.refs_7_ = bf16[4,64,640]{2,1,0:T(8,128)(2,1)S(1)} collective-permute-done((bf16[4,64,640]{2,1,0:T(8,128)(2,1)S(1)}, bf16[4,64,640]{2,1,0:T(8,128)(2,1)S(1)}, u32[]{:S(2)}, u32[]{:S(2)}) %collective-permute-start.12) | collective-permute-done | bytes 327712 | tf_op jit(solution)/shard_map/ppermute | solution.py:472
  90.9 3.3 %collective-permute-done.9.refs_3_ = bf16[4,64,640]{2,1,0:T(8,128)(2,1)S(1)} collective-permute-done((bf16[4,64,640]{2,1,0:T(8,128)(2,1)S(1)}, bf16[4,64,640]{2,1,0:T(8,128)(2,1)S(1)}, u32[]{:S(2)}, u32[]{:S(2)}) %collective-permute-start.9) | collective-permute-done | bytes 327712 | tf_op jit(solution)/shard_map/ppermute | solution.py:472
  94.2 7.7 %attend.1.a_ref.a0.a1 = bf16[1024,640]{1,0:T(8,128)(2,1)S(1)} custom-call(s32[8]{0:T(128)S(1)} %copy-done.10, s32[16]{0:T(128)S(1)} %get-tuple-element.19.info_ref, s32[4]{0:T(128)S(1)} %pad_add_fusion.place_ref, s32[8,128]{1,0:T(8,128)S(1)} %copy-done.8, f32[512,128]{1,0:T(8,128)S(1)} %norm_scales.1.r_ref, bf16[4,64,640]{2,1,0:T(8,128)(2,1)S(1)} %pad_maximum_fusion.refs_0_, ...), custom_call_target="tpu_custom_call" | custom-call | tf_op jit(solution)/shard_map/attend/pallas_call | solution.py:267
  102.0 3.0 %collective-permute-done.13.other_ref.o0.o1 = bf16[1024,640]{1,0:T(8,128)(2,1)S(1)} collective-permute-done((bf16[1024,640]{1,0:T(8,128)(2,1)S(1)}, bf16[1024,640]{1,0:T(8,128)(2,1)S(1)}, u32[]{:S(2)}, u32[]{:S(2)}) %collective-permute-start.13) | collective-permute-done | bytes 1310752 | tf_op jit(solution)/shard_map/ppermute | solution.py:509
  105.0 11.3 %all-gather.3.cloned.1.call-done = bf16[5120,640]{1,0:T(8,128)(2,1)} async-done(((bf16[320,640]{1,0:T(8,128)(2,1)}), bf16[5120,640]{1,0:T(8,128)(2,1)}) %all-gather.3.cloned.1.call-update) | async-done | bytes 6553616 | tf_op jit(solution)/shard_map/all_gather | solution.py:491
  116.3 2.9 %copy-done = bf16[5120,640]{1,0:T(8,128)(2,1)S(1)} copy-done((bf16[5120,640]{1,0:T(8,128)(2,1)S(1)}, bf16[5120,640]{1,0:T(8,128)(2,1)}, u32[]{:S(2)}) %copy-start) | copy-done | bytes 6553624
  119.2 3.4 %far_partials.1 = (bf16[512,640]{1,0:T(8,128)(2,1)S(1)}, bf16[512,640]{1,0:T(8,128)(2,1)S(1)}) custom-call(s32[4]{0:T(128)S(1)} %pad_add_fusion.place_ref, bf16[1024,640]{1,0:T(8,128)(2,1)S(1)} %attend.1.a_ref.a0.a1, bf16[1024,640]{1,0:T(8,128)(2,1)S(1)} %collective-permute-done.13.other_ref.o0.o1, bf16[16,320,640]{2,1,0:T(8,128)(2,1)S(1)} %bitcast.17, ...), custom_call_target="tpu_custom_call" | custom-call | tf_op jit(solution)/shard_map/far_partials/pallas_call | solution.py:323
  122.6 1.6 collective-permute-start.14
  124.7 3.1 %free_partials.1 = (bf16[512,640]{1,0:T(8,128)(2,1)S(1)}, bf16[512,640]{1,0:T(8,128)(2,1)S(1)}) custom-call(s32[4]{0:T(128)S(1)} %pad_add_fusion.place_ref, bf16[1024,640]{1,0:T(8,128)(2,1)S(1)} %attend.1.a_ref.a0.a1, bf16[1024,640]{1,0:T(8,128)(2,1)S(1)} %collective-permute-done.13.other_ref.o0.o1, bf16[1024,640]{1,0:T(8,128)(2,1)S(1)} %attend.1.a_ref.a0.a1, ...), custom_call_target="tpu_custom_call" | custom-call | tf_op jit(solution)/shard_map/free_partials/pallas_call | solution.py:346
  127.8 1.6 collective-permute-start.17
  129.9 10.4 %collective-permute-done.14.from_below = bf16[512,640]{1,0:T(8,128)(2,1)S(1)} collective-permute-done((bf16[512,640]{1,0:T(8,128)(2,1)S(1)}, bf16[512,640]{1,0:T(8,128)(2,1)S(1)}, u32[]{:S(2)}, u32[]{:S(2)}) %collective-permute-start.14) | collective-permute-done | bytes 655392 | tf_op jit(solution)/shard_map/ppermute | solution.py:511
  141.8 3.1 %relay_partials.1 = (bf16[512,640]{1,0:T(8,128)(2,1)S(1)}, bf16[512,640]{1,0:T(8,128)(2,1)S(1)}) custom-call(s32[4]{0:T(128)S(1)} %pad_add_fusion.place_ref, bf16[1024,640]{1,0:T(8,128)(2,1)S(1)} %attend.1.a_ref.a0.a1, bf16[1024,640]{1,0:T(8,128)(2,1)S(1)} %collective-permute-done.13.other_ref.o0.o1, bf16[1024,640]{1,0:T(8,128)(2,1)S(1)} %attend.1.a_ref.a0.a1, ...), custom_call_target="tpu_custom_call" | custom-call | tf_op jit(solution)/shard_map/relay_partials/pallas_call | solution.py:369
  147.0 1.8 %residual.1.stored_ref = bf16[8,128,640]{2,1,0:T(8,128)(2,1)S(1)} custom-call(s32[16]{0:T(128)S(1)} %get-tuple-element.19.info_ref, s32[4]{0:T(128)S(1)} %pad_add_fusion.place_ref, s32[8,128]{1,0:T(8,128)S(1)} %copy-done.8, bf16[512,5120]{1,0:T(8,128)(2,1)S(1)} %bitcast.32, bf16[128,5120]{1,0:T(8,128)(2,1)S(1)} %copy-done.3), custom_call_target="tpu_custom_call" | custom-call | flops 671088640 | bytes 2621440 | tf_op jit(solution)/shard_map/residual/pallas_call | solution.py:189
  148.9 3.3 %base_partial.1.base_ref = f32[1024,640]{1,0:T(8,128)S(1)} custom-call(s32[4]{0:T(128)S(1)} %pad_add_fusion.place_ref, bf16[1024,640]{1,0:T(8,128)(2,1)S(1)} %attend.1.a_ref.a0.a1, bf16[1024,640]{1,0:T(8,128)(2,1)S(1)} %collective-permute-done.13.other_ref.o0.o1, bf16[16,320,640]{2,1,0:T(8,128)(2,1)S(1)} %bitcast.29, bf16[16,320,640]{2,1,0:T(8,128)(2,1)S(1)} %bitcast.30), custom_call_target="tpu_custom_call" | custom-call | tf_op jit(solution)/shard_map/base_partial/pallas_call | solution.py:390
  152.2 2.2 %collective-permute-done.17.refs_1_ = bf16[512,640]{1,0:T(8,128)(2,1)S(1)} collective-permute-done((bf16[512,640]{1,0:T(8,128)(2,1)S(1)}, bf16[512,640]{1,0:T(8,128)(2,1)S(1)}, u32[]{:S(2)}, u32[]{:S(2)}) %collective-permute-start.17) | collective-permute-done | bytes 655392 | tf_op jit(solution)/shard_map/ppermute | solution.py:514
  155.8 11.6 %collective-permute-done.16.refs_0_ = bf16[512,640]{1,0:T(8,128)(2,1)S(1)} collective-permute-done((bf16[512,640]{1,0:T(8,128)(2,1)S(1)}, bf16[512,640]{1,0:T(8,128)(2,1)S(1)}, u32[]{:S(2)}, u32[]{:S(2)}) %collective-permute-start.16) | collective-permute-done | bytes 655392 | tf_op jit(solution)/shard_map/ppermute | solution.py:517
  168.7 4.0 %finish.1 = bf16[8,128,640]{2,1,0:T(8,128)(2,1)} custom-call(s32[8]{0:T(128)S(1)} %copy-done.10, s32[16]{0:T(128)S(1)} %get-tuple-element.19.info_ref, bf16[8,128,640]{2,1,0:T(8,128)(2,1)S(1)} %residual.1.stored_ref, f32[1024,640]{1,0:T(8,128)S(1)} %base_partial.1.base_ref, bf16[512,640]{1,0:T(8,128)(2,1)S(1)} %collective-permute-done.16.refs_0_, ...), custom_call_target="tpu_custom_call" | custom-call | tf_op jit(solution)/shard_map/finish/pallas_call | solution.py:432
  (65 shorter events, 20.1 us)
Async XLA Ops:
  15.1 8.1 %copy-start.12 = (bf16[640,320]{0,1:T(8,128)(2,1)S(1)}, bf16[640,320]{0,1:T(8,128)(2,1)}, u32[]{:S(2)}) copy-start(bf16[640,320]{0,1:T(8,128)(2,1)} %param.19) | copy-start | bytes 1228804
  15.1 29.5 %all-to-all-start = ((bf16[16,336,128]{2,1,0:T(8,128)(2,1)}), bf16[16,336,128]{2,1,0:T(8,128)(2,1)S(1)}, u32[]{:S(2)}, u32[]{:S(2)}) async-start(bf16[16,336,128]{2,1,0:T(8,128)(2,1)} %copy-done.4), calls=%async_computation | async-start | bytes 2752512 | tf_op jit(solution)/shard_map/all_to_all | solution.py:489
  23.1 21.5 %copy-start.2 = (bf16[128,5120]{1,0:T(8,128)(2,1)S(1)}, bf16[128,5120]{1,0:T(8,128)(2,1)}, u32[]{:S(2)}) copy-start(bf16[128,5120]{1,0:T(8,128)(2,1)} %p_ref.5) | copy-start | bytes 3932164
  23.1 93.2 %all-gather.3.cloned.1.call-start = ((), (), s32[]{:S(2)}) async-start(), calls=%async_computation.1 | async-start | bytes 6963200 | tf_op jit(solution)/shard_map/all_gather | solution.py:491
  23.1 0.9 collective-permute-start
  51.1 10.0 %collective-permute-start.4 = (bf16[64,640]{1,0:T(8,128)(2,1)S(1)}, bf16[64,640]{1,0:T(8,128)(2,1)S(1)}, u32[]{:S(2)}, u32[]{:S(2)}) collective-permute-start(bf16[64,640]{1,0:T(8,128)(2,1)S(1)} %get-tuple-element.35), channel_id=1, source_target_pairs={{0,32},{8,40},{16,48},{24,56},{32,64},{40,72},{48,80},{56,88},{64,... | collective-permute-start | bytes 245768 | tf_op jit(solution)/shard_map/ppermute | solution.py:472
  51.2 12.5 %collective-permute-start.5 = (bf16[64,640]{1,0:T(8,128)(2,1)S(1)}, bf16[64,640]{1,0:T(8,128)(2,1)S(1)}, u32[]{:S(2)}, u32[]{:S(2)}) collective-permute-start(bf16[64,640]{1,0:T(8,128)(2,1)S(1)} %get-tuple-element.35), channel_id=1, source_target_pairs={{0,64},{8,72},{16,80},{24,88},{32,96},{40,104},{48,112},{56,120},{... | collective-permute-start | bytes 245768 | tf_op jit(solution)/shard_map/ppermute | solution.py:472
  53.2 10.5 %collective-permute-start.6 = (bf16[64,640]{1,0:T(8,128)(2,1)S(1)}, bf16[64,640]{1,0:T(8,128)(2,1)S(1)}, u32[]{:S(2)}, u32[]{:S(2)}) collective-permute-start(bf16[64,640]{1,0:T(8,128)(2,1)S(1)} %get-tuple-element.35), channel_id=1, source_target_pairs={{0,96},{8,104},{16,112},{24,120},{32,0},{40,8},{48,16},{56,24},{64... | collective-permute-start | bytes 245768 | tf_op jit(solution)/shard_map/ppermute | solution.py:472
  54.8 9.8 %collective-permute-start.1 = (bf16[64,640]{1,0:T(8,128)(2,1)S(1)}, bf16[64,640]{1,0:T(8,128)(2,1)S(1)}, u32[]{:S(2)}, u32[]{:S(2)}) collective-permute-start(bf16[64,640]{1,0:T(8,128)(2,1)S(1)} %get-tuple-element.36), channel_id=1, source_target_pairs={{0,8},{8,16},{16,24},{24,0},{32,40},{40,48},{48,56},{56,32},{64,72... | collective-permute-start | bytes 245768 | tf_op jit(solution)/shard_map/ppermute | solution.py:472
  54.8 12.8 %collective-permute-start.2 = (bf16[64,640]{1,0:T(8,128)(2,1)S(1)}, bf16[64,640]{1,0:T(8,128)(2,1)S(1)}, u32[]{:S(2)}, u32[]{:S(2)}) collective-permute-start(bf16[64,640]{1,0:T(8,128)(2,1)S(1)} %get-tuple-element.36), channel_id=1, source_target_pairs={{0,16},{8,24},{16,0},{24,8},{32,48},{40,56},{48,32},{56,40},{64,80... | collective-permute-start | bytes 245768 | tf_op jit(solution)/shard_map/ppermute | solution.py:472
  61.1 6.8 %collective-permute-start.3 = (bf16[64,640]{1,0:T(8,128)(2,1)S(1)}, bf16[64,640]{1,0:T(8,128)(2,1)S(1)}, u32[]{:S(2)}, u32[]{:S(2)}) collective-permute-start(bf16[64,640]{1,0:T(8,128)(2,1)S(1)} %get-tuple-element.36), channel_id=1, source_target_pairs={{0,24},{8,0},{16,8},{24,16},{32,56},{40,32},{48,40},{56,48},{64,88... | collective-permute-start | bytes 245768 | tf_op jit(solution)/shard_map/ppermute | solution.py:472
  68.0 26.2 %copy-start.8 = (s32[8,128]{1,0:T(8,128)S(1)}, s32[8,128]{1,0:T(8,128)}, u32[]{:S(2)}) copy-start(s32[8,128]{1,0:T(8,128)} %ids_ref.3) | copy-start | bytes 12292
  68.0 26.2 %copy-start.10 = (s32[8]{0:T(128)S(1)}, s32[8]{0:T(128)}, u32[]{:S(2)}) copy-start(s32[8]{0:T(128)} %lens_ref.5) | copy-start | bytes 100
  68.0 11.4 %collective-permute-start.7 = (bf16[4,64,640]{2,1,0:T(8,128)(2,1)S(1)}, bf16[4,64,640]{2,1,0:T(8,128)(2,1)S(1)}, u32[]{:S(2)}, u32[]{:S(2)}) collective-permute-start(bf16[4,64,640]{2,1,0:T(8,128)(2,1)S(1)} %pad_maximum_fusion.refs_0_), channel_id=1, source_target_pairs={{0,32},{8,40},{16,48},{24,56},{32,64},{40,72},{48,80},{56,88},{64,... | collective-permute-start | bytes 983048 | tf_op jit(solution)/shard_map/ppermute | solution.py:472
  69.2 19.2 %collective-permute-start.10 = (bf16[4,64,640]{2,1,0:T(8,128)(2,1)S(1)}, bf16[4,64,640]{2,1,0:T(8,128)(2,1)S(1)}, u32[]{:S(2)}, u32[]{:S(2)}) collective-permute-start(bf16[4,64,640]{2,1,0:T(8,128)(2,1)S(1)} %pad_maximum_fusion.1.refs_4_), channel_id=1, source_target_pairs={{0,8},{8,16},{16,24},{24,0},{32,40},{40,48},{48,56},{56,32},{64,72... | collective-permute-start | bytes 983048 | tf_op jit(solution)/shard_map/ppermute | solution.py:472
  70.0 18.4 %collective-permute-start.11 = (bf16[4,64,640]{2,1,0:T(8,128)(2,1)S(1)}, bf16[4,64,640]{2,1,0:T(8,128)(2,1)S(1)}, u32[]{:S(2)}, u32[]{:S(2)}) collective-permute-start(bf16[4,64,640]{2,1,0:T(8,128)(2,1)S(1)} %pad_maximum_fusion.1.refs_4_), channel_id=1, source_target_pairs={{0,16},{8,24},{16,0},{24,8},{32,48},{40,56},{48,32},{56,40},{64,80... | collective-permute-start | bytes 983048 | tf_op jit(solution)/shard_map/ppermute | solution.py:472
  72.5 18.3 %collective-permute-start.12 = (bf16[4,64,640]{2,1,0:T(8,128)(2,1)S(1)}, bf16[4,64,640]{2,1,0:T(8,128)(2,1)S(1)}, u32[]{:S(2)}, u32[]{:S(2)}) collective-permute-start(bf16[4,64,640]{2,1,0:T(8,128)(2,1)S(1)} %pad_maximum_fusion.1.refs_4_), channel_id=1, source_target_pairs={{0,24},{8,0},{16,8},{24,16},{32,56},{40,32},{48,40},{56,48},{64,88... | collective-permute-start | bytes 983048 | tf_op jit(solution)/shard_map/ppermute | solution.py:472
  75.1 15.7 %collective-permute-start.8 = (bf16[4,64,640]{2,1,0:T(8,128)(2,1)S(1)}, bf16[4,64,640]{2,1,0:T(8,128)(2,1)S(1)}, u32[]{:S(2)}, u32[]{:S(2)}) collective-permute-start(bf16[4,64,640]{2,1,0:T(8,128)(2,1)S(1)} %pad_maximum_fusion.refs_0_), channel_id=1, source_target_pairs={{0,64},{8,72},{16,80},{24,88},{32,96},{40,104},{48,112},{56,120},{... | collective-permute-start | bytes 983048 | tf_op jit(solution)/shard_map/ppermute | solution.py:472
  79.4 14.8 %collective-permute-start.9 = (bf16[4,64,640]{2,1,0:T(8,128)(2,1)S(1)}, bf16[4,64,640]{2,1,0:T(8,128)(2,1)S(1)}, u32[]{:S(2)}, u32[]{:S(2)}) collective-permute-start(bf16[4,64,640]{2,1,0:T(8,128)(2,1)S(1)} %pad_maximum_fusion.refs_0_), channel_id=1, source_target_pairs={{0,96},{8,104},{16,112},{24,120},{32,0},{40,8},{48,16},{56,24},{64... | collective-permute-start | bytes 983048 | tf_op jit(solution)/shard_map/ppermute | solution.py:472
  101.9 3.1 %collective-permute-start.13 = (bf16[1024,640]{1,0:T(8,128)(2,1)S(1)}, bf16[1024,640]{1,0:T(8,128)(2,1)S(1)}, u32[]{:S(2)}, u32[]{:S(2)}) collective-permute-start(bf16[1024,640]{1,0:T(8,128)(2,1)S(1)} %attend.1.a_ref.a0.a1), channel_id=1, source_target_pairs={{0,1},{1,0},{2,3},{3,2},{4,5},{5,4},{6,7},{7,6},{8,9},{9,8},{10,11... | collective-permute-start | bytes 3932168 | tf_op jit(solution)/shard_map/ppermute | solution.py:509
  116.3 2.9 %copy-start = (bf16[5120,640]{1,0:T(8,128)(2,1)S(1)}, bf16[5120,640]{1,0:T(8,128)(2,1)}, u32[]{:S(2)}) copy-start(bf16[5120,640]{1,0:T(8,128)(2,1)} %all-gather.3.cloned.1.call-done) | copy-start | bytes 19660804
  122.6 17.7 %collective-permute-start.14 = (bf16[512,640]{1,0:T(8,128)(2,1)S(1)}, bf16[512,640]{1,0:T(8,128)(2,1)S(1)}, u32[]{:S(2)}, u32[]{:S(2)}) collective-permute-start(bf16[512,640]{1,0:T(8,128)(2,1)S(1)} %get-tuple-element.27), channel_id=1, source_target_pairs={{0,2},{1,3},{2,4},{3,5},{4,6},{5,7},{6,0},{7,1},{8,10},{9,11},{10,... | collective-permute-start | bytes 1966088 | tf_op jit(solution)/shard_map/ppermute | solution.py:511
  124.2 17.6 %collective-permute-start.15 = (bf16[512,640]{1,0:T(8,128)(2,1)S(1)}, bf16[512,640]{1,0:T(8,128)(2,1)S(1)}, u32[]{:S(2)}, u32[]{:S(2)}) collective-permute-start(bf16[512,640]{1,0:T(8,128)(2,1)S(1)} %get-tuple-element.28), channel_id=1, source_target_pairs={{0,6},{1,7},{2,0},{3,1},{4,2},{5,3},{6,4},{7,5},{8,14},{9,15},{10,... | collective-permute-start | bytes 1966088 | tf_op jit(solution)/shard_map/ppermute | solution.py:512
  124.7 22.3 %slice-start.2 = ((s8[5242880]{0:T(1024)(128)(4,1)}), s8[4194304]{0:T(1024)(128)(4,1)S(1)}, s32[]{:S(2)}) async-start(s8[5242880]{0:T(1024)(128)(4,1)} %bitcast.31), calls=%async_computation.4 | async-start | bytes 8388608
  124.7 24.1 %slice-start = ((s8[6553600]{0:T(1024)(128)(4,1)}), s8[4194304]{0:T(1024)(128)(4,1)S(1)}, s32[]{:S(2)}) async-start(s8[6553600]{0:T(1024)(128)(4,1)} %bitcast.27), calls=%async_computation.2 | async-start | bytes 8388608
  127.8 26.5 %collective-permute-start.17 = (bf16[512,640]{1,0:T(8,128)(2,1)S(1)}, bf16[512,640]{1,0:T(8,128)(2,1)S(1)}, u32[]{:S(2)}, u32[]{:S(2)}) collective-permute-start(bf16[512,640]{1,0:T(8,128)(2,1)S(1)} %get-tuple-element.30), channel_id=1, source_target_pairs={{0,2},{1,3},{2,4},{3,5},{4,6},{5,7},{6,0},{7,1},{8,10},{9,11},{10,... | collective-permute-start | bytes 1966088 | tf_op jit(solution)/shard_map/ppermute | solution.py:514
  129.3 17.6 %slice-start.3 = ((s8[5242880]{0:T(1024)(128)(4,1)}), s8[1048576]{0:T(1024)(128)(4,1)S(1)}, s32[]{:S(2)}) async-start(s8[5242880]{0:T(1024)(128)(4,1)} %bitcast.31), calls=%async_computation.5 | async-start | bytes 2097152
  129.3 17.6 %copy-start.3 = (bf16[128,5120]{1,0:T(8,128)(2,1)S(1)}, bf16[128,5120]{1,0:T(8,128)(2,1)}, u32[]{:S(2)}) copy-start(bf16[128,5120]{1,0:T(8,128)(2,1)} %p_ref.5) | copy-start | bytes 3932164
  129.3 19.5 %slice-start.1 = ((s8[6553600]{0:T(1024)(128)(4,1)}), s8[2359296]{0:T(1024)(128)(4,1)S(1)}, s32[]{:S(2)}) async-start(s8[6553600]{0:T(1024)(128)(4,1)} %bitcast.27), calls=%async_computation.3 | async-start | bytes 4718592
  129.3 26.5 %collective-permute-start.18 = (bf16[512,640]{1,0:T(8,128)(2,1)S(1)}, bf16[512,640]{1,0:T(8,128)(2,1)S(1)}, u32[]{:S(2)}, u32[]{:S(2)}) collective-permute-start(bf16[512,640]{1,0:T(8,128)(2,1)S(1)} %get-tuple-element.31), channel_id=1, source_target_pairs={{0,6},{1,7},{2,0},{3,1},{4,2},{5,3},{6,4},{7,5},{8,14},{9,15},{10,... | collective-permute-start | bytes 1966088 | tf_op jit(solution)/shard_map/ppermute | solution.py:515
  144.9 22.6 %collective-permute-start.16 = (bf16[512,640]{1,0:T(8,128)(2,1)S(1)}, bf16[512,640]{1,0:T(8,128)(2,1)S(1)}, u32[]{:S(2)}, u32[]{:S(2)}) collective-permute-start(bf16[512,640]{1,0:T(8,128)(2,1)S(1)} %get-tuple-element.29), channel_id=1, source_target_pairs={{0,2},{1,3},{2,4},{3,5},{4,6},{5,7},{6,0},{7,1},{8,10},{9,11},{10,... | collective-permute-start | bytes 1966088 | tf_op jit(solution)/shard_map/ppermute | solution.py:517
  146.1 22.5 %collective-permute-start.19 = (bf16[512,640]{1,0:T(8,128)(2,1)S(1)}, bf16[512,640]{1,0:T(8,128)(2,1)S(1)}, u32[]{:S(2)}, u32[]{:S(2)}) collective-permute-start(bf16[512,640]{1,0:T(8,128)(2,1)S(1)} %get-tuple-element.32), channel_id=1, source_target_pairs={{0,6},{1,7},{2,0},{3,1},{4,2},{5,3},{6,4},{7,5},{8,14},{9,15},{10,... | collective-permute-start | bytes 1966088 | tf_op jit(solution)/shard_map/ppermute | solution.py:518
  (7 other events, 7.9 us)
Sparse Core Ops, SparseCore 0:
  44.7 71.6 all-gather.2
where the time goes:
time: 180 us
  waiting for transfers between devices  80.3 us (45%)
  Pallas kernels  36.9 us (20%)
  starting transfers between devices  36.1 us (20%)
  between operations  13.7 us (8%)
  local copies, waits for them, and re-layouts  11.6 us (6%)
    ppermute x12, starting transfers between devices, spread(): lax.ppermute(value, 'row', shifted(o, along_x))  20.8 us
    all_to_all x1, waiting for transfers between devices, on_device(): w_block = lax.all_to_all(packed, 'row', 0, 0)  19.7 us
    ppermute x12, waiting for transfers between devices, spread(): lax.ppermute(value, 'row', shifted(o, along_x))  17.9 us
    ppermute x1, waiting for transfers between devices, rest(): below_high = lax.ppermute(up, 'mp', along(1))  11.6 us
    all_gather x1, waiting for transfers between devices, on_device(): w_all = lax.all_gather(tiles, 'row', axis=0)  11.3 us
    unnamed x34, local copies, waits for them, and re-layouts  10.8 us
    ppermute x1, waiting for transfers between devices, rest(): from_below = lax.ppermute(top, 'mp', along(1))  10.4 us
    all_to_all x1, starting transfers between devices, on_device(): w_block = lax.all_to_all(packed, 'row', 0, 0)  8.01 us
  transfers between devices with their start and end apart: 22, of which 16 were waited for; matrix products, arithmetic and copies ran while one was open for 1% of the time, Pallas kernels for 15%

commit v1 on v0

--- a/solution.py
+++ b/solution.py
@@ -20,9 +20,8 @@
 F32 = jnp.float32
 BF16 = jnp.bfloat16
 VMEM = 16 << 20
-NOTE = 16
+MOST = 57 << 20
 GROUP = 16
-CAPACITIES = (640, 704, 768, 832, 896, SLOTS * SEQ)
 
 
 def mm(a, b, dims):
@@ -48,15 +47,12 @@
     turned_ref[...] = line.T
     start = pl.multiple_of((row % 2) * BLOCK, 8)
     gain = turned_ref[pl.ds(start, BLOCK), :][:, :1]
-    out_ref[ROWS - 1, :BLOCK] = jnp.zeros((BLOCK, DH), BF16)
-    count = jnp.full((NOTE, DH), total, jnp.int32).astype(F32).astype(BF16)
-    for i in range(ROWS):
-        out_ref[i, BLOCK:] = count
+    out_ref[ROWS - 1] = jnp.zeros((BLOCK, DH), BF16)
     for j, copy in enumerate(copies):
         copy.wait()
         for h in range(HEADS):
             block = gain * w_ref[j, :, DH * h : DH * (h + 1)].astype(F32)
-            out_ref[HEADS * j + h, :BLOCK] = block.astype(BF16)
+            out_ref[HEADS * j + h] = block.astype(BF16)
 
 
 def pack(place, lengths, counts, gain, w_query, w_key, w_value):
@@ -68,7 +64,7 @@
             grid=(1,),
             in_specs=[pl.BlockSpec((8, 2 * BLOCK), lambda i, *_: (0, 0)), stay, stay, stay],
             out_specs=[
-                pl.BlockSpec((ROWS, BLOCK + NOTE, DH), lambda i, *_: (0, 0, 0)),
+                pl.BlockSpec((ROWS, BLOCK, DH), lambda i, *_: (0, 0, 0)),
                 pl.BlockSpec(memory_space=pltpu.SMEM),
             ],
             scratch_shapes=[
@@ -78,10 +74,10 @@
             ],
         ),
         out_shape=[
-            jax.ShapeDtypeStruct((ROWS, BLOCK + NOTE, DH), BF16),
+            jax.ShapeDtypeStruct((ROWS, BLOCK, DH), BF16),
             jax.ShapeDtypeStruct((2 * SLOTS,), jnp.int32),
         ],
-        compiler_params=pltpu.CompilerParams(vmem_limit_bytes=VMEM),
+        compiler_params=pltpu.CompilerParams(vmem_limit_bytes=MOST),
         name="pack",
     )(place, lengths, counts, gain, w_query, w_key, w_value)
 
@@ -93,7 +89,7 @@
     def _():
         t_acc[...] = jnp.zeros_like(t_acc)
 
-    w = w_ref[:, :BLOCK].reshape(2 * BLOCK, DH)
+    w = w_ref[...].reshape(2 * BLOCK, DH)
     t_acc[:, :VOCAB] += mm(w, e_ref[...], ((0,), (1,)))
     t_acc[:, VOCAB:] += mm(w, p_ref[...], ((0,), (1,)))
 
@@ -109,7 +105,7 @@
         in_specs=[
             pl.BlockSpec((VOCAB, 2 * BLOCK), lambda k: (0, k)),
             pl.BlockSpec((SEQ, 2 * BLOCK), lambda k: (0, k)),
-            pl.BlockSpec((2, BLOCK + NOTE, DH), lambda k: (k, 0, 0)),
+            pl.BlockSpec((2, BLOCK, DH), lambda k: (k, 0, 0)),
         ],
         out_specs=pl.BlockSpec((DH, TABLE), lambda k: (0, 0)),
         out_shape=jax.ShapeDtypeStruct((DH, TABLE), BF16),
@@ -472,6 +468,10 @@
         near = {o: lax.ppermute(value, "row", shifted(o, along_x)) for o in (1, 3, 2)}
         return [value, near[1], near[2], near[3]]
 
+    packed, info = pack(
+        place, set_lengths, live_counts, norm_gain.reshape(8, 2 * BLOCK), w_query, w_key, w_value
+    )
+    packed, w_out, embed_late = lax.optimization_barrier((packed, w_out, embed_table))
     turned = w_out.T
     cross = []
     for z in range(SIDE):
@@ -482,23 +482,18 @@
                 cross.append((source, (SIDE * z + 3 - x) * 8 + 2 * line + 1 - c))
     crossed = lax.ppermute(turned, ("row", "mp"), cross)
     tiles = jnp.where((row % SIDE) // 2 == core, turned, crossed)
-
-    packed, info = pack(
-        place, set_lengths, live_counts, norm_gain.reshape(8, 2 * BLOCK), w_query, w_key, w_value
-    )
+    r = norm_scales(embed_late, position_table)
     w_block = lax.all_to_all(packed, "row", 0, 0)
-    w_block, tiles = lax.optimization_barrier((w_block, tiles))
+    w_block, tiles, r = lax.optimization_barrier((w_block, tiles, r))
     w_all = lax.all_gather(tiles, "row", axis=0)
-    most = GROUP * jnp.max(w_block[:, BLOCK, 0].astype(F32)).astype(jnp.int32)
     mine = project_tables(embed_table, position_table, w_block)
 
     a_line = jnp.stack(spread(mine[:HALF], True))
     b_line = jnp.stack(spread(mine[HALF:], False))
     a_line, b_line = lax.optimization_barrier((a_line, b_line))
     a_parts, b_parts = spread(a_line, False), spread(b_line, True)
-    embed_late, a_parts[1] = lax.optimization_barrier((embed_table, a_parts[1]))
-    r = norm_scales(embed_late, position_table)
-
+    ids_late, a_parts[1] = lax.optimization_barrier((token_ids, a_parts[1]))
+    stored = residual(info, place, ids_late, embed_table, position_table)
     swap = [(2 * i + c, 2 * i + 1 - c) for i in range(SIDE) for c in range(2)]
 
     def along(o):
@@ -517,7 +512,6 @@
         below_high = lax.ppermute(up, "mp", along(1))
         above_low = lax.ppermute(down, "mp", along(3))
         base = base_partial(place, mixed, other, w)
-        stored = residual(info, place, token_ids, embed_table, position_table)
         return finish(
             set_lengths, info, stored, base, (below_high, below_low), (above_high, above_low)
         )

time: 180 us -> 178 us (0.989)
  waiting for transfers between devices: 80.3 us -> 76.8 us
  local copies, waits for them, and re-layouts: 11.6 us -> 9.24 us
  Pallas kernels: 36.9 us -> 38.7 us
    all_to_all x1, waiting for transfers between devices: 19.7 us -> 11.6 us  [on_device(): w_block = lax.all_to_all(packed, 'row', 0, 0)]
    ppermute x12, waiting for transfers between devices: 17.9 us -> 22.8 us  [spread(): lax.ppermute(value, 'row', shifted(o, along_x))]
    unnamed x34 -> x28, local copies, waits for them, and re-layouts: 10.8 us -> 7.88 us
  transfers between devices with their start and end apart: 22 -> 22, of which waited for: 16 -> 16; matrix products, arithmetic and copies ran while one was open for 1% -> 1% of each run, Pallas kernels for 15% -> 16%
where the time goes in v1:
time: 178 us; the launch traced here: 177 us
  waiting for transfers between devices  76.8 us (43%)
  Pallas kernels  38.7 us (22%)
  starting transfers between devices  37.1 us (21%)
  between operations  13.6 us (8%)
  local copies, waits for them, and re-layouts  9.24 us (5%)
    ppermute x12, waiting for transfers between devices, spread(): lax.ppermute(value, 'row', shifted(o, along_x))  22.8 us
    ppermute x12, starting transfers between devices, spread(): lax.ppermute(value, 'row', shifted(o, along_x))  21.2 us
    all_to_all x1, waiting for transfers between devices, on_device(): w_block = lax.all_to_all(packed, 'row', 0, 0)  11.6 us
    ppermute x1, waiting for transfers between devices, rest(): below_high = lax.ppermute(up, 'mp', along(1))  11.6 us
    all_gather x1, waiting for transfers between devices, on_device(): w_all = lax.all_gather(tiles, 'row', axis=0)  11.1 us
    ppermute x1, waiting for transfers between devices, rest(): from_below = lax.ppermute(top, 'mp', along(1))  10.4 us
    all_to_all x1, starting transfers between devices, on_device(): w_block = lax.all_to_all(packed, 'row', 0, 0)  8.02 us
    unnamed x28, local copies, waits for them, and re-layouts  7.88 us
  transfers between devices with their start and end apart: 22, of which 16 were waited for; matrix products, arithmetic and copies ran while one was open for 1% of the time, Pallas kernels for 16%

profile of v1, /device:TPU:8, one launch (start us, length us, event | category | flops | bytes accessed | tf_op | source)
XLA Modules:
  0.0 177.0 jit_solution(6308784108064631960)
XLA Ops:
  8.5 3.9 %pack.1 = (bf16[16,320,128]{2,1,0:T(8,128)(2,1)}, s32[16]{0:T(128)}) custom-call(s32[4]{0:T(128)} %pad_add_fusion.place_ref, s32[8]{0:T(128)} %lens_ref.5, s32[16]{0:T(128)} %counts_ref.1, f32[8,640]{1,0:T(8,128)} %reshape.3.gain_ref, bf16[320,640]{1,0:T(8,128)(2,1)} %q_hbm.1, bf16[320,640]{1,0:T(8,128)(2,1)} %k_hbm.1, bf16[320,640]{1,0:T(8,128)(2,1)} %v_hbm.1), custom_call_target="tpu_custom_call" | custom-call | tf_op jit(solution)/shard_map/pack/pallas_call | solution.py:60
  12.4 8.0 %all-to-all-start = ((bf16[16,320,128]{2,1,0:T(8,128)(2,1)}), bf16[16,320,128]{2,1,0:T(8,128)(2,1)S(1)}, u32[]{:S(2)}, u32[]{:S(2)}) async-start(bf16[16,320,128]{2,1,0:T(8,128)(2,1)} %get-tuple-element.25), calls=%async_computation | async-start | bytes 2621440 | tf_op jit(solution)/shard_map/all_to_all | solution.py:486
  21.9 2.5 %copy-done.1 = bf16[512,5120]{1,0:T(8,128)(2,1)S(1)} copy-done((bf16[512,5120]{1,0:T(8,128)(2,1)S(1)}, bf16[512,5120]{1,0:T(8,128)(2,1)}, u32[]{:S(2)}) %copy-start.1) | copy-done | bytes 5242904
  24.4 4.2 %norm_scales.1.r_ref = f32[512,128]{1,0:T(8,128)S(1)} custom-call(bf16[512,5120]{1,0:T(8,128)(2,1)S(1)} %copy-done.1, bf16[128,5120]{1,0:T(8,128)(2,1)S(1)} %copy-done.3), custom_call_target="tpu_custom_call" | custom-call | flops 838860800 | bytes 6553600 | tf_op jit(solution)/shard_map/norm_scales/pallas_call | solution.py:149
  29.3 11.6 %all-to-all-done.w_ref = bf16[16,320,128]{2,1,0:T(8,128)(2,1)S(1)} async-done(((bf16[16,320,128]{2,1,0:T(8,128)(2,1)}), bf16[16,320,128]{2,1,0:T(8,128)(2,1)S(1)}, u32[]{:S(2)}, u32[]{:S(2)}) %all-to-all-start) | async-done | bytes 1310752 | tf_op jit(solution)/shard_map/all_to_all | solution.py:486
  41.0 2.5 %copy-done.2 = bf16[512,5120]{1,0:T(8,128)(2,1)S(1)} copy-done((bf16[512,5120]{1,0:T(8,128)(2,1)S(1)}, bf16[512,5120]{1,0:T(8,128)(2,1)}, u32[]{:S(2)}) %copy-start.2) | copy-done | bytes 5242904
  43.5 4.0 %project_tables.1 = bf16[128,640]{1,0:T(8,128)(2,1)S(1)} custom-call(bf16[512,5120]{1,0:T(8,128)(2,1)S(1)} %copy-done.2, bf16[128,5120]{1,0:T(8,128)(2,1)S(1)} %copy-done.3, bf16[16,320,128]{2,1,0:T(8,128)(2,1)S(1)} %all-to-all-done.w_ref), custom_call_target="tpu_custom_call" | custom-call | tf_op jit(solution)/shard_map/project_tables/pallas_call | solution.py:102
  47.7 1.8 %collective-permute-start.5 = (bf16[64,640]{1,0:T(8,128)(2,1)S(1)}, bf16[64,640]{1,0:T(8,128)(2,1)S(1)}, u32[]{:S(2)}, u32[]{:S(2)}) collective-permute-start(bf16[64,640]{1,0:T(8,128)(2,1)S(1)} %get-tuple-element.43), channel_id=1, source_target_pairs={{0,64},{8,72},{16,80},{24,88},{32,96},{40,104},{48,112},{56,120},{... | collective-permute-start | bytes 245768 | tf_op jit(solution)/shard_map/ppermute | solution.py:468
  49.5 1.8 %collective-permute-start.6 = (bf16[64,640]{1,0:T(8,128)(2,1)S(1)}, bf16[64,640]{1,0:T(8,128)(2,1)S(1)}, u32[]{:S(2)}, u32[]{:S(2)}) collective-permute-start(bf16[64,640]{1,0:T(8,128)(2,1)S(1)} %get-tuple-element.43), channel_id=1, source_target_pairs={{0,96},{8,104},{16,112},{24,120},{32,0},{40,8},{48,16},{56,24},{64... | collective-permute-start | bytes 245768 | tf_op jit(solution)/shard_map/ppermute | solution.py:468
  51.3 7.3 %collective-permute-start.2 = (bf16[64,640]{1,0:T(8,128)(2,1)S(1)}, bf16[64,640]{1,0:T(8,128)(2,1)S(1)}, u32[]{:S(2)}, u32[]{:S(2)}) collective-permute-start(bf16[64,640]{1,0:T(8,128)(2,1)S(1)} %get-tuple-element.44), channel_id=1, source_target_pairs={{0,16},{8,24},{16,0},{24,8},{32,48},{40,56},{48,32},{56,40},{64,80... | collective-permute-start | bytes 245768 | tf_op jit(solution)/shard_map/ppermute | solution.py:468
  58.6 2.6 %collective-permute-start.3 = (bf16[64,640]{1,0:T(8,128)(2,1)S(1)}, bf16[64,640]{1,0:T(8,128)(2,1)S(1)}, u32[]{:S(2)}, u32[]{:S(2)}) collective-permute-start(bf16[64,640]{1,0:T(8,128)(2,1)S(1)} %get-tuple-element.44), channel_id=1, source_target_pairs={{0,24},{8,0},{16,8},{24,16},{32,56},{40,32},{48,40},{56,48},{64,88... | collective-permute-start | bytes 245768 | tf_op jit(solution)/shard_map/ppermute | solution.py:468
  62.9 2.2 %collective-permute-done.2 = bf16[64,640]{1,0:T(8,128)(2,1)S(1)} collective-permute-done((bf16[64,640]{1,0:T(8,128)(2,1)S(1)}, bf16[64,640]{1,0:T(8,128)(2,1)S(1)}, u32[]{:S(2)}, u32[]{:S(2)}) %collective-permute-start.2) | collective-permute-done | bytes 81952 | tf_op jit(solution)/shard_map/ppermute | solution.py:468
  67.5 2.5 %collective-permute-start.11 = (bf16[4,64,640]{2,1,0:T(8,128)(2,1)S(1)}, bf16[4,64,640]{2,1,0:T(8,128)(2,1)S(1)}, u32[]{:S(2)}, u32[]{:S(2)}) collective-permute-start(bf16[4,64,640]{2,1,0:T(8,128)(2,1)S(1)} %pad_maximum_fusion.1.refs_4_), channel_id=1, source_target_pairs={{0,16},{8,24},{16,0},{24,8},{32,48},{40,56},{48,32},{56,40},{64,80... | collective-permute-start | bytes 983048 | tf_op jit(solution)/shard_map/ppermute | solution.py:468
  70.0 2.6 %collective-permute-start.12 = (bf16[4,64,640]{2,1,0:T(8,128)(2,1)S(1)}, bf16[4,64,640]{2,1,0:T(8,128)(2,1)S(1)}, u32[]{:S(2)}, u32[]{:S(2)}) collective-permute-start(bf16[4,64,640]{2,1,0:T(8,128)(2,1)S(1)} %pad_maximum_fusion.1.refs_4_), channel_id=1, source_target_pairs={{0,24},{8,0},{16,8},{24,16},{32,56},{40,32},{48,40},{56,48},{64,88... | collective-permute-start | bytes 983048 | tf_op jit(solution)/shard_map/ppermute | solution.py:468
  72.6 4.6 %collective-permute-done.7.refs_1_ = bf16[4,64,640]{2,1,0:T(8,128)(2,1)S(1)} collective-permute-done((bf16[4,64,640]{2,1,0:T(8,128)(2,1)S(1)}, bf16[4,64,640]{2,1,0:T(8,128)(2,1)S(1)}, u32[]{:S(2)}, u32[]{:S(2)}) %collective-permute-start.7) | collective-permute-done | bytes 327712 | tf_op jit(solution)/shard_map/ppermute | solution.py:468
  78.0 8.4 %collective-permute-done.10.refs_5_ = bf16[4,64,640]{2,1,0:T(8,128)(2,1)S(1)} collective-permute-done((bf16[4,64,640]{2,1,0:T(8,128)(2,1)S(1)}, bf16[4,64,640]{2,1,0:T(8,128)(2,1)S(1)}, u32[]{:S(2)}, u32[]{:S(2)}) %collective-permute-start.10) | collective-permute-done | bytes 327712 | tf_op jit(solution)/shard_map/ppermute | solution.py:468
  86.4 2.5 %collective-permute-done.12.refs_7_ = bf16[4,64,640]{2,1,0:T(8,128)(2,1)S(1)} collective-permute-done((bf16[4,64,640]{2,1,0:T(8,128)(2,1)S(1)}, bf16[4,64,640]{2,1,0:T(8,128)(2,1)S(1)}, u32[]{:S(2)}, u32[]{:S(2)}) %collective-permute-start.12) | collective-permute-done | bytes 327712 | tf_op jit(solution)/shard_map/ppermute | solution.py:468
  88.8 3.0 %collective-permute-done.9.refs_3_ = bf16[4,64,640]{2,1,0:T(8,128)(2,1)S(1)} collective-permute-done((bf16[4,64,640]{2,1,0:T(8,128)(2,1)S(1)}, bf16[4,64,640]{2,1,0:T(8,128)(2,1)S(1)}, u32[]{:S(2)}, u32[]{:S(2)}) %collective-permute-start.9) | collective-permute-done | bytes 327712 | tf_op jit(solution)/shard_map/ppermute | solution.py:468
  91.8 7.7 %attend.1.a_ref.a0.a1 = bf16[1024,640]{1,0:T(8,128)(2,1)S(1)} custom-call(s32[8]{0:T(128)S(1)} %copy-done.7, s32[16]{0:T(128)S(1)} %copy-done.8, s32[4]{0:T(128)S(1)} %copy-done.5, s32[8,128]{1,0:T(8,128)S(1)} %copy-done.6, f32[512,128]{1,0:T(8,128)S(1)} %norm_scales.1.r_ref, bf16[4,64,640]{2,1,0:T(8,128)(2,1)S(1)} %pad_maximum_fusion.refs_0_, ...), custom_call_target="tpu_custom_call" | custom-call | tf_op jit(solution)/shard_map/attend/pallas_call | solution.py:263
  99.7 3.0 %collective-permute-done.13.other_ref.o0.o1 = bf16[1024,640]{1,0:T(8,128)(2,1)S(1)} collective-permute-done((bf16[1024,640]{1,0:T(8,128)(2,1)S(1)}, bf16[1024,640]{1,0:T(8,128)(2,1)S(1)}, u32[]{:S(2)}, u32[]{:S(2)}) %collective-permute-start.13) | collective-permute-done | bytes 1310752 | tf_op jit(solution)/shard_map/ppermute | solution.py:504
  102.7 11.1 %all-gather.3.cloned.1.call-done = bf16[5120,640]{1,0:T(8,128)(2,1)} async-done(((bf16[320,640]{1,0:T(8,128)(2,1)}), bf16[5120,640]{1,0:T(8,128)(2,1)}) %all-gather.3.cloned.1.call-update) | async-done | bytes 6553616 | tf_op jit(solution)/shard_map/all_gather | solution.py:488
  113.8 2.9 %copy-done = bf16[5120,640]{1,0:T(8,128)(2,1)S(1)} copy-done((bf16[5120,640]{1,0:T(8,128)(2,1)S(1)}, bf16[5120,640]{1,0:T(8,128)(2,1)}, u32[]{:S(2)}) %copy-start) | copy-done | bytes 6553624
  116.7 3.4 %far_partials.1 = (bf16[512,640]{1,0:T(8,128)(2,1)S(1)}, bf16[512,640]{1,0:T(8,128)(2,1)S(1)}) custom-call(s32[4]{0:T(128)S(1)} %copy-done.5, bf16[1024,640]{1,0:T(8,128)(2,1)S(1)} %attend.1.a_ref.a0.a1, bf16[1024,640]{1,0:T(8,128)(2,1)S(1)} %collective-permute-done.13.other_ref.o0.o1, bf16[16,320,640]{2,1,0:T(8,128)(2,1)S(1)} %bitcast.17, ...), custom_call_target="tpu_custom_call" | custom-call | tf_op jit(solution)/shard_map/far_partials/pallas_call | solution.py:319
  122.2 3.1 %free_partials.1 = (bf16[512,640]{1,0:T(8,128)(2,1)S(1)}, bf16[512,640]{1,0:T(8,128)(2,1)S(1)}) custom-call(s32[4]{0:T(128)S(1)} %copy-done.5, bf16[1024,640]{1,0:T(8,128)(2,1)S(1)} %attend.1.a_ref.a0.a1, bf16[1024,640]{1,0:T(8,128)(2,1)S(1)} %collective-permute-done.13.other_ref.o0.o1, bf16[1024,640]{1,0:T(8,128)(2,1)S(1)} %attend.1.a_ref.a0.a1, ...), custom_call_target="tpu_custom_call" | custom-call | tf_op jit(solution)/shard_map/free_partials/pallas_call | solution.py:342
  125.3 1.6 collective-permute-start.17
  127.4 10.4 %collective-permute-done.14.from_below = bf16[512,640]{1,0:T(8,128)(2,1)S(1)} collective-permute-done((bf16[512,640]{1,0:T(8,128)(2,1)S(1)}, bf16[512,640]{1,0:T(8,128)(2,1)S(1)}, u32[]{:S(2)}, u32[]{:S(2)}) %collective-permute-start.14) | collective-permute-done | bytes 655392 | tf_op jit(solution)/shard_map/ppermute | solution.py:506
  139.3 3.1 %relay_partials.1 = (bf16[512,640]{1,0:T(8,128)(2,1)S(1)}, bf16[512,640]{1,0:T(8,128)(2,1)S(1)}) custom-call(s32[4]{0:T(128)S(1)} %copy-done.5, bf16[1024,640]{1,0:T(8,128)(2,1)S(1)} %attend.1.a_ref.a0.a1, bf16[1024,640]{1,0:T(8,128)(2,1)S(1)} %collective-permute-done.13.other_ref.o0.o1, bf16[1024,640]{1,0:T(8,128)(2,1)S(1)} %attend.1.a_ref.a0.a1, ...), custom_call_target="tpu_custom_call" | custom-call | tf_op jit(solution)/shard_map/relay_partials/pallas_call | solution.py:365
  144.5 2.1 %residual.1.stored_ref = bf16[8,128,640]{2,1,0:T(8,128)(2,1)S(1)} custom-call(s32[16]{0:T(128)S(1)} %copy-done.8, s32[4]{0:T(128)S(1)} %copy-done.5, s32[8,128]{1,0:T(8,128)S(1)} %copy-done.6, bf16[512,5120]{1,0:T(8,128)(2,1)S(1)} %bitcast.32, bf16[128,5120]{1,0:T(8,128)(2,1)S(1)} %copy-done.4), custom_call_target="tpu_custom_call" | custom-call | flops 671088640 | bytes 2621440 | tf_op jit(solution)/shard_map/residual/pallas_call | solution.py:185
  146.6 3.3 %base_partial.1.base_ref = f32[1024,640]{1,0:T(8,128)S(1)} custom-call(s32[4]{0:T(128)S(1)} %copy-done.5, bf16[1024,640]{1,0:T(8,128)(2,1)S(1)} %attend.1.a_ref.a0.a1, bf16[1024,640]{1,0:T(8,128)(2,1)S(1)} %collective-permute-done.13.other_ref.o0.o1, bf16[16,320,640]{2,1,0:T(8,128)(2,1)S(1)} %bitcast.29, bf16[16,320,640]{2,1,0:T(8,128)(2,1)S(1)} %bitcast.30), custom_call_target="tpu_custom_call" | custom-call | tf_op jit(solution)/shard_map/base_partial/pallas_call | solution.py:386
  149.9 1.9 %collective-permute-done.17.refs_1_ = bf16[512,640]{1,0:T(8,128)(2,1)S(1)} collective-permute-done((bf16[512,640]{1,0:T(8,128)(2,1)S(1)}, bf16[512,640]{1,0:T(8,128)(2,1)S(1)}, u32[]{:S(2)}, u32[]{:S(2)}) %collective-permute-start.17) | collective-permute-done | bytes 655392 | tf_op jit(solution)/shard_map/ppermute | solution.py:509
  153.3 11.6 %collective-permute-done.16.refs_0_ = bf16[512,640]{1,0:T(8,128)(2,1)S(1)} collective-permute-done((bf16[512,640]{1,0:T(8,128)(2,1)S(1)}, bf16[512,640]{1,0:T(8,128)(2,1)S(1)}, u32[]{:S(2)}, u32[]{:S(2)}) %collective-permute-start.16) | collective-permute-done | bytes 655392 | tf_op jit(solution)/shard_map/ppermute | solution.py:512
  166.2 4.0 %finish.1 = bf16[8,128,640]{2,1,0:T(8,128)(2,1)} custom-call(s32[8]{0:T(128)S(1)} %copy-done.7, s32[16]{0:T(128)S(1)} %copy-done.8, bf16[8,128,640]{2,1,0:T(8,128)(2,1)S(1)} %residual.1.stored_ref, f32[1024,640]{1,0:T(8,128)S(1)} %base_partial.1.base_ref, bf16[512,640]{1,0:T(8,128)(2,1)S(1)} %collective-permute-done.16.refs_0_, ...), custom_call_target="tpu_custom_call" | custom-call | tf_op jit(solution)/shard_map/finish/pallas_call | solution.py:428
  (59 shorter events, 18.4 us)
Async XLA Ops:
  12.4 9.5 %copy-start.3 = (bf16[128,5120]{1,0:T(8,128)(2,1)S(1)}, bf16[128,5120]{1,0:T(8,128)(2,1)}, u32[]{:S(2)}) copy-start(bf16[128,5120]{1,0:T(8,128)(2,1)} %p_ref.5) | copy-start | bytes 3932164
  12.4 28.6 %all-to-all-start = ((bf16[16,320,128]{2,1,0:T(8,128)(2,1)}), bf16[16,320,128]{2,1,0:T(8,128)(2,1)S(1)}, u32[]{:S(2)}, u32[]{:S(2)}) async-start(bf16[16,320,128]{2,1,0:T(8,128)(2,1)} %get-tuple-element.25), calls=%async_computation | async-start | bytes 2621440 | tf_op jit(solution)/shard_map/all_to_all | solution.py:486
  20.4 93.4 %all-gather.3.cloned.1.call-start = ((), (), s32[]{:S(2)}) async-start(), calls=%async_computation.1 | async-start | bytes 6963200 | tf_op jit(solution)/shard_map/all_gather | solution.py:488
  20.5 8.1 %collective-permute-start = (bf16[320,640]{1,0:T(8,128)(2,1)S(1)}, bf16[320,640]{1,0:T(8,128)(2,1)}, u32[]{:S(2)}, u32[]{:S(2)}) collective-permute-start(bf16[320,640]{1,0:T(8,128)(2,1)S(1)} %bitcast.33), channel_id=1, source_target_pairs={{1,24},{3,26},{5,28},{7,30},{9,16},{11,18},{13,20},{15,22},{16,9},... | collective-permute-start | bytes 1228808 | tf_op jit(solution)/shard_map/ppermute | solution.py:483
  47.5 44.3 %copy-start.5 = (s32[4]{0:T(128)S(1)}, s32[4]{0:T(128)}, u32[]{:S(2)}) copy-start(s32[4]{0:T(128)} %pad_add_fusion.place_ref) | copy-start | bytes 52
  47.5 44.3 %copy-start.6 = (s32[8,128]{1,0:T(8,128)S(1)}, s32[8,128]{1,0:T(8,128)}, u32[]{:S(2)}) copy-start(s32[8,128]{1,0:T(8,128)} %ids_ref.2) | copy-start | bytes 12292
  47.5 44.3 %copy-start.7 = (s32[8]{0:T(128)S(1)}, s32[8]{0:T(128)}, u32[]{:S(2)}) copy-start(s32[8]{0:T(128)} %lens_ref.5) | copy-start | bytes 100
  47.5 44.3 %copy-start.8 = (s32[16]{0:T(128)S(1)}, s32[16]{0:T(128)}, u32[]{:S(2)}) copy-start(s32[16]{0:T(128)} %get-tuple-element.23.info_ref) | copy-start | bytes 196
  47.6 11.0 %collective-permute-start.4 = (bf16[64,640]{1,0:T(8,128)(2,1)S(1)}, bf16[64,640]{1,0:T(8,128)(2,1)S(1)}, u32[]{:S(2)}, u32[]{:S(2)}) collective-permute-start(bf16[64,640]{1,0:T(8,128)(2,1)S(1)} %get-tuple-element.43), channel_id=1, source_target_pairs={{0,32},{8,40},{16,48},{24,56},{32,64},{40,72},{48,80},{56,88},{64,... | collective-permute-start | bytes 245768 | tf_op jit(solution)/shard_map/ppermute | solution.py:468
  47.7 13.6 %collective-permute-start.5 = (bf16[64,640]{1,0:T(8,128)(2,1)S(1)}, bf16[64,640]{1,0:T(8,128)(2,1)S(1)}, u32[]{:S(2)}, u32[]{:S(2)}) collective-permute-start(bf16[64,640]{1,0:T(8,128)(2,1)S(1)} %get-tuple-element.43), channel_id=1, source_target_pairs={{0,64},{8,72},{16,80},{24,88},{32,96},{40,104},{48,112},{56,120},{... | collective-permute-start | bytes 245768 | tf_op jit(solution)/shard_map/ppermute | solution.py:468
  49.5 11.7 %collective-permute-start.6 = (bf16[64,640]{1,0:T(8,128)(2,1)S(1)}, bf16[64,640]{1,0:T(8,128)(2,1)S(1)}, u32[]{:S(2)}, u32[]{:S(2)}) collective-permute-start(bf16[64,640]{1,0:T(8,128)(2,1)S(1)} %get-tuple-element.43), channel_id=1, source_target_pairs={{0,96},{8,104},{16,112},{24,120},{32,0},{40,8},{48,16},{56,24},{64... | collective-permute-start | bytes 245768 | tf_op jit(solution)/shard_map/ppermute | solution.py:468
  51.3 11.6 %collective-permute-start.1 = (bf16[64,640]{1,0:T(8,128)(2,1)S(1)}, bf16[64,640]{1,0:T(8,128)(2,1)S(1)}, u32[]{:S(2)}, u32[]{:S(2)}) collective-permute-start(bf16[64,640]{1,0:T(8,128)(2,1)S(1)} %get-tuple-element.44), channel_id=1, source_target_pairs={{0,8},{8,16},{16,24},{24,0},{32,40},{40,48},{48,56},{56,32},{64,72... | collective-permute-start | bytes 245768 | tf_op jit(solution)/shard_map/ppermute | solution.py:468
  51.3 13.8 %collective-permute-start.2 = (bf16[64,640]{1,0:T(8,128)(2,1)S(1)}, bf16[64,640]{1,0:T(8,128)(2,1)S(1)}, u32[]{:S(2)}, u32[]{:S(2)}) collective-permute-start(bf16[64,640]{1,0:T(8,128)(2,1)S(1)} %get-tuple-element.44), channel_id=1, source_target_pairs={{0,16},{8,24},{16,0},{24,8},{32,48},{40,56},{48,32},{56,40},{64,80... | collective-permute-start | bytes 245768 | tf_op jit(solution)/shard_map/ppermute | solution.py:468
  58.6 7.1 %collective-permute-start.3 = (bf16[64,640]{1,0:T(8,128)(2,1)S(1)}, bf16[64,640]{1,0:T(8,128)(2,1)S(1)}, u32[]{:S(2)}, u32[]{:S(2)}) collective-permute-start(bf16[64,640]{1,0:T(8,128)(2,1)S(1)} %get-tuple-element.44), channel_id=1, source_target_pairs={{0,24},{8,0},{16,8},{24,16},{32,56},{40,32},{48,40},{56,48},{64,88... | collective-permute-start | bytes 245768 | tf_op jit(solution)/shard_map/ppermute | solution.py:468
  65.8 11.4 %collective-permute-start.7 = (bf16[4,64,640]{2,1,0:T(8,128)(2,1)S(1)}, bf16[4,64,640]{2,1,0:T(8,128)(2,1)S(1)}, u32[]{:S(2)}, u32[]{:S(2)}) collective-permute-start(bf16[4,64,640]{2,1,0:T(8,128)(2,1)S(1)} %pad_maximum_fusion.refs_0_), channel_id=1, source_target_pairs={{0,32},{8,40},{16,48},{24,56},{32,64},{40,72},{48,80},{56,88},{64,... | collective-permute-start | bytes 983048 | tf_op jit(solution)/shard_map/ppermute | solution.py:468
  66.7 19.6 %collective-permute-start.10 = (bf16[4,64,640]{2,1,0:T(8,128)(2,1)S(1)}, bf16[4,64,640]{2,1,0:T(8,128)(2,1)S(1)}, u32[]{:S(2)}, u32[]{:S(2)}) collective-permute-start(bf16[4,64,640]{2,1,0:T(8,128)(2,1)S(1)} %pad_maximum_fusion.1.refs_4_), channel_id=1, source_target_pairs={{0,8},{8,16},{16,24},{24,0},{32,40},{40,48},{48,56},{56,32},{64,72... | collective-permute-start | bytes 983048 | tf_op jit(solution)/shard_map/ppermute | solution.py:468
  67.5 18.8 %collective-permute-start.11 = (bf16[4,64,640]{2,1,0:T(8,128)(2,1)S(1)}, bf16[4,64,640]{2,1,0:T(8,128)(2,1)S(1)}, u32[]{:S(2)}, u32[]{:S(2)}) collective-permute-start(bf16[4,64,640]{2,1,0:T(8,128)(2,1)S(1)} %pad_maximum_fusion.1.refs_4_), channel_id=1, source_target_pairs={{0,16},{8,24},{16,0},{24,8},{32,48},{40,56},{48,32},{56,40},{64,80... | collective-permute-start | bytes 983048 | tf_op jit(solution)/shard_map/ppermute | solution.py:468
  70.0 18.8 %collective-permute-start.12 = (bf16[4,64,640]{2,1,0:T(8,128)(2,1)S(1)}, bf16[4,64,640]{2,1,0:T(8,128)(2,1)S(1)}, u32[]{:S(2)}, u32[]{:S(2)}) collective-permute-start(bf16[4,64,640]{2,1,0:T(8,128)(2,1)S(1)} %pad_maximum_fusion.1.refs_4_), channel_id=1, source_target_pairs={{0,24},{8,0},{16,8},{24,16},{32,56},{40,32},{48,40},{56,48},{64,88... | collective-permute-start | bytes 983048 | tf_op jit(solution)/shard_map/ppermute | solution.py:468
  72.6 16.2 %collective-permute-start.8 = (bf16[4,64,640]{2,1,0:T(8,128)(2,1)S(1)}, bf16[4,64,640]{2,1,0:T(8,128)(2,1)S(1)}, u32[]{:S(2)}, u32[]{:S(2)}) collective-permute-start(bf16[4,64,640]{2,1,0:T(8,128)(2,1)S(1)} %pad_maximum_fusion.refs_0_), channel_id=1, source_target_pairs={{0,64},{8,72},{16,80},{24,88},{32,96},{40,104},{48,112},{56,120},{... | collective-permute-start | bytes 983048 | tf_op jit(solution)/shard_map/ppermute | solution.py:468
  77.2 14.6 %collective-permute-start.9 = (bf16[4,64,640]{2,1,0:T(8,128)(2,1)S(1)}, bf16[4,64,640]{2,1,0:T(8,128)(2,1)S(1)}, u32[]{:S(2)}, u32[]{:S(2)}) collective-permute-start(bf16[4,64,640]{2,1,0:T(8,128)(2,1)S(1)} %pad_maximum_fusion.refs_0_), channel_id=1, source_target_pairs={{0,96},{8,104},{16,112},{24,120},{32,0},{40,8},{48,16},{56,24},{64... | collective-permute-start | bytes 983048 | tf_op jit(solution)/shard_map/ppermute | solution.py:468
  99.6 3.1 %collective-permute-start.13 = (bf16[1024,640]{1,0:T(8,128)(2,1)S(1)}, bf16[1024,640]{1,0:T(8,128)(2,1)S(1)}, u32[]{:S(2)}, u32[]{:S(2)}) collective-permute-start(bf16[1024,640]{1,0:T(8,128)(2,1)S(1)} %attend.1.a_ref.a0.a1), channel_id=1, source_target_pairs={{0,1},{1,0},{2,3},{3,2},{4,5},{5,4},{6,7},{7,6},{8,9},{9,8},{10,11... | collective-permute-start | bytes 3932168 | tf_op jit(solution)/shard_map/ppermute | solution.py:504
  120.1 17.7 %collective-permute-start.14 = (bf16[512,640]{1,0:T(8,128)(2,1)S(1)}, bf16[512,640]{1,0:T(8,128)(2,1)S(1)}, u32[]{:S(2)}, u32[]{:S(2)}) collective-permute-start(bf16[512,640]{1,0:T(8,128)(2,1)S(1)} %get-tuple-element.35), channel_id=1, source_target_pairs={{0,2},{1,3},{2,4},{3,5},{4,6},{5,7},{6,0},{7,1},{8,10},{9,11},{10,... | collective-permute-start | bytes 1966088 | tf_op jit(solution)/shard_map/ppermute | solution.py:506
  121.7 17.6 %collective-permute-start.15 = (bf16[512,640]{1,0:T(8,128)(2,1)S(1)}, bf16[512,640]{1,0:T(8,128)(2,1)S(1)}, u32[]{:S(2)}, u32[]{:S(2)}) collective-permute-start(bf16[512,640]{1,0:T(8,128)(2,1)S(1)} %get-tuple-element.36), channel_id=1, source_target_pairs={{0,6},{1,7},{2,0},{3,1},{4,2},{5,3},{6,4},{7,5},{8,14},{9,15},{10,... | collective-permute-start | bytes 1966088 | tf_op jit(solution)/shard_map/ppermute | solution.py:507
  122.2 22.3 %slice-start.2 = ((s8[5242880]{0:T(1024)(128)(4,1)}), s8[4194304]{0:T(1024)(128)(4,1)S(1)}, s32[]{:S(2)}) async-start(s8[5242880]{0:T(1024)(128)(4,1)} %bitcast.31), calls=%async_computation.4 | async-start | bytes 8388608
  122.2 24.4 %slice-start = ((s8[6553600]{0:T(1024)(128)(4,1)}), s8[4194304]{0:T(1024)(128)(4,1)S(1)}, s32[]{:S(2)}) async-start(s8[6553600]{0:T(1024)(128)(4,1)} %bitcast.27), calls=%async_computation.2 | async-start | bytes 8388608
  125.3 26.5 %collective-permute-start.17 = (bf16[512,640]{1,0:T(8,128)(2,1)S(1)}, bf16[512,640]{1,0:T(8,128)(2,1)S(1)}, u32[]{:S(2)}, u32[]{:S(2)}) collective-permute-start(bf16[512,640]{1,0:T(8,128)(2,1)S(1)} %get-tuple-element.38), channel_id=1, source_target_pairs={{0,2},{1,3},{2,4},{3,5},{4,6},{5,7},{6,0},{7,1},{8,10},{9,11},{10,... | collective-permute-start | bytes 1966088 | tf_op jit(solution)/shard_map/ppermute | solution.py:509
  126.8 17.6 %slice-start.3 = ((s8[5242880]{0:T(1024)(128)(4,1)}), s8[1048576]{0:T(1024)(128)(4,1)S(1)}, s32[]{:S(2)}) async-start(s8[5242880]{0:T(1024)(128)(4,1)} %bitcast.31), calls=%async_computation.5 | async-start | bytes 2097152
  126.8 17.6 %copy-start.4 = (bf16[128,5120]{1,0:T(8,128)(2,1)S(1)}, bf16[128,5120]{1,0:T(8,128)(2,1)}, u32[]{:S(2)}) copy-start(bf16[128,5120]{1,0:T(8,128)(2,1)} %p_ref.5) | copy-start | bytes 3932164
  126.8 19.8 %slice-start.1 = ((s8[6553600]{0:T(1024)(128)(4,1)}), s8[2359296]{0:T(1024)(128)(4,1)S(1)}, s32[]{:S(2)}) async-start(s8[6553600]{0:T(1024)(128)(4,1)} %bitcast.27), calls=%async_computation.3 | async-start | bytes 4718592
  126.8 26.5 %collective-permute-start.18 = (bf16[512,640]{1,0:T(8,128)(2,1)S(1)}, bf16[512,640]{1,0:T(8,128)(2,1)S(1)}, u32[]{:S(2)}, u32[]{:S(2)}) collective-permute-start(bf16[512,640]{1,0:T(8,128)(2,1)S(1)} %get-tuple-element.39), channel_id=1, source_target_pairs={{0,6},{1,7},{2,0},{3,1},{4,2},{5,3},{6,4},{7,5},{8,14},{9,15},{10,... | collective-permute-start | bytes 1966088 | tf_op jit(solution)/shard_map/ppermute | solution.py:510
  142.4 22.6 %collective-permute-start.16 = (bf16[512,640]{1,0:T(8,128)(2,1)S(1)}, bf16[512,640]{1,0:T(8,128)(2,1)S(1)}, u32[]{:S(2)}, u32[]{:S(2)}) collective-permute-start(bf16[512,640]{1,0:T(8,128)(2,1)S(1)} %get-tuple-element.37), channel_id=1, source_target_pairs={{0,2},{1,3},{2,4},{3,5},{4,6},{5,7},{6,0},{7,1},{8,10},{9,11},{10,... | collective-permute-start | bytes 1966088 | tf_op jit(solution)/shard_map/ppermute | solution.py:512
  143.6 22.5 %collective-permute-start.19 = (bf16[512,640]{1,0:T(8,128)(2,1)S(1)}, bf16[512,640]{1,0:T(8,128)(2,1)S(1)}, u32[]{:S(2)}, u32[]{:S(2)}) collective-permute-start(bf16[512,640]{1,0:T(8,128)(2,1)S(1)} %get-tuple-element.40), channel_id=1, source_target_pairs={{0,6},{1,7},{2,0},{3,1},{4,2},{5,3},{6,4},{7,5},{8,14},{9,15},{10,... | collective-permute-start | bytes 1966088 | tf_op jit(solution)/shard_map/ppermute | solution.py:513
  (4 other events, 15.9 us)
Sparse Core Ops, SparseCore 0:
  41.1 72.6 all-gather.2

commit v2 on v1

--- a/solution.py
+++ b/solution.py
@@ -203,7 +203,7 @@
 
 def attend_kernel(lens_ref, info_ref, place_ref, ids_ref, r_ref, *refs):
     a_refs, b_refs = refs[:SIDE], refs[SIDE : 2 * SIDE]
-    out_ref, table_ref, set_ref = refs[2 * SIDE :]
+    out_ref, table_ref = refs[2 * SIDE :]
     step = pl.program_id(0)
     z, x = place_ref[0] // SIDE, place_ref[0] % SIDE
 
@@ -214,6 +214,9 @@
                 source = SIDE * ((z + SIDE - dz) % SIDE) + (x + SIDE - dx) % SIDE
                 table_ref[pl.ds(source, 1), :HALF] = a_refs[dz][dx : dx + 1]
                 table_ref[pl.ds(source, 1), HALF:] = b_refs[dx][dz : dz + 1]
+
+    @pl.when(2 * step >= info_ref[SLOTS])
+    def _():
         out_ref[...] = jnp.zeros_like(out_ref)
 
     @pl.when(2 * step < info_ref[SLOTS])
@@ -248,14 +251,7 @@
                 expo = jnp.exp(scores - jnp.max(scores, axis=0, keepdims=True))
                 weights = (expo / jnp.sum(expo, axis=0, keepdims=True)).astype(BF16)
                 mixed = mm(v, weights, ((1,), (0,)))
-                set_ref[s, :, DH * h : DH * (h + 1)] = mixed.T.astype(BF16)
-        for s in range(2):
-            for i in range(SEQ // GROUP):
-
-                @pl.when((2 * step + s < info_ref[SLOTS]) & (GROUP * i < lens_ref[2 * step + s]))
-                def _(s=s, i=i):
-                    at = pl.multiple_of(info_ref[2 * step + s] + GROUP * i, GROUP)
-                    out_ref[pl.ds(at, GROUP), :] = set_ref[s, GROUP * i : GROUP * (i + 1), :]
+                out_ref[cols, DH * h : DH * (h + 1)] = mixed.T.astype(BF16)
 
 
 def attend(capacity, lengths, info, place, ids, r, a_parts, b_parts):
@@ -270,10 +266,9 @@
                 pl.BlockSpec((VOCAB, SEQ), lambda i, *_: (0, 0)),
                 *[quarter] * (2 * SIDE),
             ],
-            out_specs=pl.BlockSpec((capacity, FEATURES), lambda i, *_: (0, 0)),
+            out_specs=pl.BlockSpec((2 * SEQ, FEATURES), lambda i, *_: (i, 0)),
             scratch_shapes=[
                 pltpu.VMEM((ROWS, DH, TABLE), BF16),
-                pltpu.VMEM((2, SEQ, FEATURES), BF16),
             ],
         ),
         out_shape=jax.ShapeDtypeStruct((capacity, FEATURES), BF16),
@@ -400,37 +395,32 @@
 def finish_kernel(lens_ref, info_ref, stored_ref, base_ref, *refs):
     below, above, out_ref = refs[:2], refs[2:4], refs[4]
     slot = pl.program_id(0)
-    tile = below[0].shape[0]
-    for i in range(SEQ // GROUP):
-        here = slice(GROUP * i, GROUP * (i + 1))
-        live = (slot < info_ref[SLOTS]) & (GROUP * i < lens_ref[slot])
-        start = pl.multiple_of(info_ref[slot] + GROUP * i, GROUP)
-        for half in range(2):
-
-            @pl.when(live & ((start >= tile) if half else (start < tile)))
-            def _(i=i, here=here, half=half, start=start):
-                at = pl.ds(pl.multiple_of(start - half * tile, GROUP), GROUP)
-                total = base_ref[pl.ds(start, GROUP), :] + below[half][at, :].astype(F32)
-                total += above[half][at, :].astype(F32)
-                place = GROUP * i + lax.broadcasted_iota(jnp.int32, (GROUP, FEATURES), 0)
-                result = stored_ref[0, here].astype(F32) + total
-                out_ref[0, here] = jnp.where(place < lens_ref[slot], result, 0.0).astype(BF16)
-
-        @pl.when(jnp.logical_not(live))
-        def _(here=here):
-            out_ref[0, here] = jnp.zeros((GROUP, FEATURES), BF16)
+    live = slot < info_ref[SLOTS]
+    for half in range(2):
+        here = (slot >= SLOTS // 2) if half else (slot < SLOTS // 2)
+
+        @pl.when(live & here)
+        def _(half=half):
+            total = base_ref[...] + below[half][...].astype(F32) + above[half][...].astype(F32)
+            valid = lax.broadcasted_iota(jnp.int32, (SEQ, FEATURES), 0) < lens_ref[slot]
+            result = stored_ref[0].astype(F32) + total
+            out_ref[0] = jnp.where(valid, result, 0.0).astype(BF16)
+
+    @pl.when(jnp.logical_not(live))
+    def _():
+        out_ref[...] = jnp.zeros_like(out_ref)
 
 
 def finish(lengths, info, stored, base, below, above):
-    whole = pl.BlockSpec(base.shape, lambda s, *_: (0, 0))
-    half = pl.BlockSpec(below[0].shape, lambda s, *_: (0, 0))
+    high = pl.BlockSpec((SEQ, FEATURES), lambda s, *_: (jnp.minimum(s, SLOTS // 2 - 1), 0))
+    low = pl.BlockSpec((SEQ, FEATURES), lambda s, *_: (jnp.maximum(s - SLOTS // 2, 0), 0))
     one = pl.BlockSpec((1, SEQ, FEATURES), lambda s, *_: (s, 0, 0))
     return pl.pallas_call(
         finish_kernel,
         grid_spec=pltpu.PrefetchScalarGridSpec(
             num_scalar_prefetch=2,
             grid=(SLOTS,),
-            in_specs=[one, whole, half, half, half, half],
+            in_specs=[one, pl.BlockSpec((SEQ, FEATURES), lambda s, *_: (s, 0)), high, low, high, low],
             out_specs=one,
         ),
         out_shape=jax.ShapeDtypeStruct((SLOTS, SEQ, FEATURES), BF16),

time: 178 us -> 177 us (level)
  Pallas kernels: 38.7 us -> 34.2 us
  waiting for transfers between devices: 76.8 us -> 80.8 us
    all_gather x1, waiting for transfers between devices: 11.1 us -> 14.6 us  [on_device(): w_all = lax.all_gather(tiles, 'row', axis=0)]
    pallas_call x1, Pallas kernels: 7.74 us -> 4.22 us  [attend(): pl.pallas_call(attend_kernel, grid_spec=pltpu.PrefetchScalarGridSpec(num_...]
  transfers between devices with their start and end apart: 22 -> 22, of which waited for: 16 -> 16; matrix products, arithmetic and copies ran while one was open for 1% -> 1% of each run, Pallas kernels for 16% -> 13%
where the time goes in v2:
time: 177 us
  waiting for transfers between devices  80.8 us (46%)
  starting transfers between devices  37.1 us (21%)
  Pallas kernels  34.2 us (19%)
  between operations  13.6 us (8%)
  local copies, waits for them, and re-layouts  9.24 us (5%)
    ppermute x12, waiting for transfers between devices, spread(): lax.ppermute(value, 'row', shifted(o, along_x))  22.8 us
    ppermute x12, starting transfers between devices, spread(): lax.ppermute(value, 'row', shifted(o, along_x))  21.2 us
    all_gather x1, waiting for transfers between devices, on_device(): w_all = lax.all_gather(tiles, 'row', axis=0)  14.6 us
    all_to_all x1, waiting for transfers between devices, on_device(): w_block = lax.all_to_all(packed, 'row', 0, 0)  11.6 us
    ppermute x1, waiting for transfers between devices, rest(): below_high = lax.ppermute(up, 'mp', along(1))  11.6 us
    ppermute x1, waiting for transfers between devices, rest(): from_below = lax.ppermute(top, 'mp', along(1))  10.4 us
    all_to_all x1, starting transfers between devices, on_device(): w_block = lax.all_to_all(packed, 'row', 0, 0)  8.02 us
    unnamed x28, local copies, waits for them, and re-layouts  7.88 us
  transfers between devices with their start and end apart: 22, of which 16 were waited for; matrix products, arithmetic and copies ran while one was open for 1% of the time, Pallas kernels for 13%

profile of v2, /device:TPU:8, one launch (start us, length us, event | category | flops | bytes accessed | tf_op | source)
XLA Modules:
  0.0 176.5 jit_solution(5951291252067828633)
XLA Ops:
  8.5 3.9 %pack.1 = (bf16[16,320,128]{2,1,0:T(8,128)(2,1)}, s32[16]{0:T(128)}) custom-call(s32[4]{0:T(128)} %pad_add_fusion.place_ref, s32[8]{0:T(128)} %lens_ref.5, s32[16]{0:T(128)} %counts_ref.1, f32[8,640]{1,0:T(8,128)} %reshape.3.gain_ref, bf16[320,640]{1,0:T(8,128)(2,1)} %q_hbm.1, bf16[320,640]{1,0:T(8,128)(2,1)} %k_hbm.1, bf16[320,640]{1,0:T(8,128)(2,1)} %v_hbm.1), custom_call_target="tpu_custom_call" | custom-call | tf_op jit(solution)/shard_map/pack/pallas_call | solution.py:60
  12.4 8.0 %all-to-all-start = ((bf16[16,320,128]{2,1,0:T(8,128)(2,1)}), bf16[16,320,128]{2,1,0:T(8,128)(2,1)S(1)}, u32[]{:S(2)}, u32[]{:S(2)}) async-start(bf16[16,320,128]{2,1,0:T(8,128)(2,1)} %get-tuple-element.25), calls=%async_computation | async-start | bytes 2621440 | tf_op jit(solution)/shard_map/all_to_all | solution.py:476
  21.9 2.5 %copy-done.1 = bf16[512,5120]{1,0:T(8,128)(2,1)S(1)} copy-done((bf16[512,5120]{1,0:T(8,128)(2,1)S(1)}, bf16[512,5120]{1,0:T(8,128)(2,1)}, u32[]{:S(2)}) %copy-start.1) | copy-done | bytes 5242904
  24.4 4.2 %norm_scales.1.r_ref = f32[512,128]{1,0:T(8,128)S(1)} custom-call(bf16[512,5120]{1,0:T(8,128)(2,1)S(1)} %copy-done.1, bf16[128,5120]{1,0:T(8,128)(2,1)S(1)} %copy-done.3), custom_call_target="tpu_custom_call" | custom-call | flops 838860800 | bytes 6553600 | tf_op jit(solution)/shard_map/norm_scales/pallas_call | solution.py:149
  29.3 11.6 %all-to-all-done.w_ref = bf16[16,320,128]{2,1,0:T(8,128)(2,1)S(1)} async-done(((bf16[16,320,128]{2,1,0:T(8,128)(2,1)}), bf16[16,320,128]{2,1,0:T(8,128)(2,1)S(1)}, u32[]{:S(2)}, u32[]{:S(2)}) %all-to-all-start) | async-done | bytes 1310752 | tf_op jit(solution)/shard_map/all_to_all | solution.py:476
  41.0 2.5 %copy-done.2 = bf16[512,5120]{1,0:T(8,128)(2,1)S(1)} copy-done((bf16[512,5120]{1,0:T(8,128)(2,1)S(1)}, bf16[512,5120]{1,0:T(8,128)(2,1)}, u32[]{:S(2)}) %copy-start.2) | copy-done | bytes 5242904
  43.5 4.0 %project_tables.1 = bf16[128,640]{1,0:T(8,128)(2,1)S(1)} custom-call(bf16[512,5120]{1,0:T(8,128)(2,1)S(1)} %copy-done.2, bf16[128,5120]{1,0:T(8,128)(2,1)S(1)} %copy-done.3, bf16[16,320,128]{2,1,0:T(8,128)(2,1)S(1)} %all-to-all-done.w_ref), custom_call_target="tpu_custom_call" | custom-call | tf_op jit(solution)/shard_map/project_tables/pallas_call | solution.py:102
  47.7 1.8 %collective-permute-start.5 = (bf16[64,640]{1,0:T(8,128)(2,1)S(1)}, bf16[64,640]{1,0:T(8,128)(2,1)S(1)}, u32[]{:S(2)}, u32[]{:S(2)}) collective-permute-start(bf16[64,640]{1,0:T(8,128)(2,1)S(1)} %get-tuple-element.43), channel_id=1, source_target_pairs={{0,64},{8,72},{16,80},{24,88},{32,96},{40,104},{48,112},{56,120},{... | collective-permute-start | bytes 245768 | tf_op jit(solution)/shard_map/ppermute | solution.py:458
  49.5 1.8 %collective-permute-start.6 = (bf16[64,640]{1,0:T(8,128)(2,1)S(1)}, bf16[64,640]{1,0:T(8,128)(2,1)S(1)}, u32[]{:S(2)}, u32[]{:S(2)}) collective-permute-start(bf16[64,640]{1,0:T(8,128)(2,1)S(1)} %get-tuple-element.43), channel_id=1, source_target_pairs={{0,96},{8,104},{16,112},{24,120},{32,0},{40,8},{48,16},{56,24},{64... | collective-permute-start | bytes 245768 | tf_op jit(solution)/shard_map/ppermute | solution.py:458
  51.3 7.3 %collective-permute-start.2 = (bf16[64,640]{1,0:T(8,128)(2,1)S(1)}, bf16[64,640]{1,0:T(8,128)(2,1)S(1)}, u32[]{:S(2)}, u32[]{:S(2)}) collective-permute-start(bf16[64,640]{1,0:T(8,128)(2,1)S(1)} %get-tuple-element.44), channel_id=1, source_target_pairs={{0,16},{8,24},{16,0},{24,8},{32,48},{40,56},{48,32},{56,40},{64,80... | collective-permute-start | bytes 245768 | tf_op jit(solution)/shard_map/ppermute | solution.py:458
  58.6 2.6 %collective-permute-start.3 = (bf16[64,640]{1,0:T(8,128)(2,1)S(1)}, bf16[64,640]{1,0:T(8,128)(2,1)S(1)}, u32[]{:S(2)}, u32[]{:S(2)}) collective-permute-start(bf16[64,640]{1,0:T(8,128)(2,1)S(1)} %get-tuple-element.44), channel_id=1, source_target_pairs={{0,24},{8,0},{16,8},{24,16},{32,56},{40,32},{48,40},{56,48},{64,88... | collective-permute-start | bytes 245768 | tf_op jit(solution)/shard_map/ppermute | solution.py:458
  62.9 2.2 %collective-permute-done.2 = bf16[64,640]{1,0:T(8,128)(2,1)S(1)} collective-permute-done((bf16[64,640]{1,0:T(8,128)(2,1)S(1)}, bf16[64,640]{1,0:T(8,128)(2,1)S(1)}, u32[]{:S(2)}, u32[]{:S(2)}) %collective-permute-start.2) | collective-permute-done | bytes 81952 | tf_op jit(solution)/shard_map/ppermute | solution.py:458
  67.5 2.5 %collective-permute-start.11 = (bf16[4,64,640]{2,1,0:T(8,128)(2,1)S(1)}, bf16[4,64,640]{2,1,0:T(8,128)(2,1)S(1)}, u32[]{:S(2)}, u32[]{:S(2)}) collective-permute-start(bf16[4,64,640]{2,1,0:T(8,128)(2,1)S(1)} %pad_maximum_fusion.1.refs_4_), channel_id=1, source_target_pairs={{0,16},{8,24},{16,0},{24,8},{32,48},{40,56},{48,32},{56,40},{64,80... | collective-permute-start | bytes 983048 | tf_op jit(solution)/shard_map/ppermute | solution.py:458
  70.0 2.6 %collective-permute-start.12 = (bf16[4,64,640]{2,1,0:T(8,128)(2,1)S(1)}, bf16[4,64,640]{2,1,0:T(8,128)(2,1)S(1)}, u32[]{:S(2)}, u32[]{:S(2)}) collective-permute-start(bf16[4,64,640]{2,1,0:T(8,128)(2,1)S(1)} %pad_maximum_fusion.1.refs_4_), channel_id=1, source_target_pairs={{0,24},{8,0},{16,8},{24,16},{32,56},{40,32},{48,40},{56,48},{64,88... | collective-permute-start | bytes 983048 | tf_op jit(solution)/shard_map/ppermute | solution.py:458
  72.6 4.6 %collective-permute-done.7.refs_1_ = bf16[4,64,640]{2,1,0:T(8,128)(2,1)S(1)} collective-permute-done((bf16[4,64,640]{2,1,0:T(8,128)(2,1)S(1)}, bf16[4,64,640]{2,1,0:T(8,128)(2,1)S(1)}, u32[]{:S(2)}, u32[]{:S(2)}) %collective-permute-start.7) | collective-permute-done | bytes 327712 | tf_op jit(solution)/shard_map/ppermute | solution.py:458
  78.0 8.4 %collective-permute-done.10.refs_5_ = bf16[4,64,640]{2,1,0:T(8,128)(2,1)S(1)} collective-permute-done((bf16[4,64,640]{2,1,0:T(8,128)(2,1)S(1)}, bf16[4,64,640]{2,1,0:T(8,128)(2,1)S(1)}, u32[]{:S(2)}, u32[]{:S(2)}) %collective-permute-start.10) | collective-permute-done | bytes 327712 | tf_op jit(solution)/shard_map/ppermute | solution.py:458
  86.4 2.5 %collective-permute-done.12.refs_7_ = bf16[4,64,640]{2,1,0:T(8,128)(2,1)S(1)} collective-permute-done((bf16[4,64,640]{2,1,0:T(8,128)(2,1)S(1)}, bf16[4,64,640]{2,1,0:T(8,128)(2,1)S(1)}, u32[]{:S(2)}, u32[]{:S(2)}) %collective-permute-start.12) | collective-permute-done | bytes 327712 | tf_op jit(solution)/shard_map/ppermute | solution.py:458
  88.8 3.0 %collective-permute-done.9.refs_3_ = bf16[4,64,640]{2,1,0:T(8,128)(2,1)S(1)} collective-permute-done((bf16[4,64,640]{2,1,0:T(8,128)(2,1)S(1)}, bf16[4,64,640]{2,1,0:T(8,128)(2,1)S(1)}, u32[]{:S(2)}, u32[]{:S(2)}) %collective-permute-start.9) | collective-permute-done | bytes 327712 | tf_op jit(solution)/shard_map/ppermute | solution.py:458
  91.8 4.2 %attend.1.a_ref.a0.a1 = bf16[1024,640]{1,0:T(8,128)(2,1)S(1)} custom-call(s32[8]{0:T(128)S(1)} %copy-done.7, s32[16]{0:T(128)S(1)} %copy-done.8, s32[4]{0:T(128)S(1)} %copy-done.5, s32[8,128]{1,0:T(8,128)S(1)} %copy-done.6, f32[512,128]{1,0:T(8,128)S(1)} %norm_scales.1.r_ref, bf16[4,64,640]{2,1,0:T(8,128)(2,1)S(1)} %pad_maximum_fusion.refs_0_, ...), custom_call_target="tpu_custom_call" | custom-call | tf_op jit(solution)/shard_map/attend/pallas_call | solution.py:259
  96.2 3.0 %collective-permute-done.13.other_ref.o0.o1 = bf16[1024,640]{1,0:T(8,128)(2,1)S(1)} collective-permute-done((bf16[1024,640]{1,0:T(8,128)(2,1)S(1)}, bf16[1024,640]{1,0:T(8,128)(2,1)S(1)}, u32[]{:S(2)}, u32[]{:S(2)}) %collective-permute-start.13) | collective-permute-done | bytes 1310752 | tf_op jit(solution)/shard_map/ppermute | solution.py:494
  99.2 14.6 %all-gather.3.cloned.1.call-done = bf16[5120,640]{1,0:T(8,128)(2,1)} async-done(((bf16[320,640]{1,0:T(8,128)(2,1)}), bf16[5120,640]{1,0:T(8,128)(2,1)}) %all-gather.3.cloned.1.call-update) | async-done | bytes 6553616 | tf_op jit(solution)/shard_map/all_gather | solution.py:478
  113.8 2.9 %copy-done = bf16[5120,640]{1,0:T(8,128)(2,1)S(1)} copy-done((bf16[5120,640]{1,0:T(8,128)(2,1)S(1)}, bf16[5120,640]{1,0:T(8,128)(2,1)}, u32[]{:S(2)}) %copy-start) | copy-done | bytes 6553624
  116.7 3.4 %far_partials.1 = (bf16[512,640]{1,0:T(8,128)(2,1)S(1)}, bf16[512,640]{1,0:T(8,128)(2,1)S(1)}) custom-call(s32[4]{0:T(128)S(1)} %copy-done.5, bf16[1024,640]{1,0:T(8,128)(2,1)S(1)} %attend.1.a_ref.a0.a1, bf16[1024,640]{1,0:T(8,128)(2,1)S(1)} %collective-permute-done.13.other_ref.o0.o1, bf16[16,320,640]{2,1,0:T(8,128)(2,1)S(1)} %bitcast.17, ...), custom_call_target="tpu_custom_call" | custom-call | tf_op jit(solution)/shard_map/far_partials/pallas_call | solution.py:314
  122.2 3.1 %free_partials.1 = (bf16[512,640]{1,0:T(8,128)(2,1)S(1)}, bf16[512,640]{1,0:T(8,128)(2,1)S(1)}) custom-call(s32[4]{0:T(128)S(1)} %copy-done.5, bf16[1024,640]{1,0:T(8,128)(2,1)S(1)} %attend.1.a_ref.a0.a1, bf16[1024,640]{1,0:T(8,128)(2,1)S(1)} %collective-permute-done.13.other_ref.o0.o1, bf16[1024,640]{1,0:T(8,128)(2,1)S(1)} %attend.1.a_ref.a0.a1, ...), custom_call_target="tpu_custom_call" | custom-call | tf_op jit(solution)/shard_map/free_partials/pallas_call | solution.py:337
  125.3 1.6 collective-permute-start.17
  127.4 10.4 %collective-permute-done.14.from_below = bf16[512,640]{1,0:T(8,128)(2,1)S(1)} collective-permute-done((bf16[512,640]{1,0:T(8,128)(2,1)S(1)}, bf16[512,640]{1,0:T(8,128)(2,1)S(1)}, u32[]{:S(2)}, u32[]{:S(2)}) %collective-permute-start.14) | collective-permute-done | bytes 655392 | tf_op jit(solution)/shard_map/ppermute | solution.py:496
  139.3 3.1 %relay_partials.1 = (bf16[512,640]{1,0:T(8,128)(2,1)S(1)}, bf16[512,640]{1,0:T(8,128)(2,1)S(1)}) custom-call(s32[4]{0:T(128)S(1)} %copy-done.5, bf16[1024,640]{1,0:T(8,128)(2,1)S(1)} %attend.1.a_ref.a0.a1, bf16[1024,640]{1,0:T(8,128)(2,1)S(1)} %collective-permute-done.13.other_ref.o0.o1, bf16[1024,640]{1,0:T(8,128)(2,1)S(1)} %attend.1.a_ref.a0.a1, ...), custom_call_target="tpu_custom_call" | custom-call | tf_op jit(solution)/shard_map/relay_partials/pallas_call | solution.py:360
  144.5 1.6 residual.1.stored_ref
  146.1 3.3 %base_partial.1.base_ref = f32[1024,640]{1,0:T(8,128)S(1)} custom-call(s32[4]{0:T(128)S(1)} %copy-done.5, bf16[1024,640]{1,0:T(8,128)(2,1)S(1)} %attend.1.a_ref.a0.a1, bf16[1024,640]{1,0:T(8,128)(2,1)S(1)} %collective-permute-done.13.other_ref.o0.o1, bf16[16,320,640]{2,1,0:T(8,128)(2,1)S(1)} %bitcast.29, bf16[16,320,640]{2,1,0:T(8,128)(2,1)S(1)} %bitcast.30), custom_call_target="tpu_custom_call" | custom-call | tf_op jit(solution)/shard_map/base_partial/pallas_call | solution.py:381
  149.4 2.4 %collective-permute-done.17.refs_1_ = bf16[512,640]{1,0:T(8,128)(2,1)S(1)} collective-permute-done((bf16[512,640]{1,0:T(8,128)(2,1)S(1)}, bf16[512,640]{1,0:T(8,128)(2,1)S(1)}, u32[]{:S(2)}, u32[]{:S(2)}) %collective-permute-start.17) | collective-permute-done | bytes 655392 | tf_op jit(solution)/shard_map/ppermute | solution.py:499
  153.3 11.6 %collective-permute-done.16.refs_0_ = bf16[512,640]{1,0:T(8,128)(2,1)S(1)} collective-permute-done((bf16[512,640]{1,0:T(8,128)(2,1)S(1)}, bf16[512,640]{1,0:T(8,128)(2,1)S(1)}, u32[]{:S(2)}, u32[]{:S(2)}) %collective-permute-start.16) | collective-permute-done | bytes 655392 | tf_op jit(solution)/shard_map/ppermute | solution.py:502
  166.2 3.5 %finish.1 = bf16[8,128,640]{2,1,0:T(8,128)(2,1)} custom-call(s32[8]{0:T(128)S(1)} %copy-done.7, s32[16]{0:T(128)S(1)} %copy-done.8, bf16[8,128,640]{2,1,0:T(8,128)(2,1)S(1)} %residual.1.stored_ref, f32[1024,640]{1,0:T(8,128)S(1)} %base_partial.1.base_ref, bf16[512,640]{1,0:T(8,128)(2,1)S(1)} %collective-permute-done.16.refs_0_, ...), custom_call_target="tpu_custom_call" | custom-call | tf_op jit(solution)/shard_map/finish/pallas_call | solution.py:418
  (59 shorter events, 18.4 us)
Async XLA Ops:
  12.4 9.5 %copy-start.3 = (bf16[128,5120]{1,0:T(8,128)(2,1)S(1)}, bf16[128,5120]{1,0:T(8,128)(2,1)}, u32[]{:S(2)}) copy-start(bf16[128,5120]{1,0:T(8,128)(2,1)} %p_ref.5) | copy-start | bytes 3932164
  12.4 28.6 %all-to-all-start = ((bf16[16,320,128]{2,1,0:T(8,128)(2,1)}), bf16[16,320,128]{2,1,0:T(8,128)(2,1)S(1)}, u32[]{:S(2)}, u32[]{:S(2)}) async-start(bf16[16,320,128]{2,1,0:T(8,128)(2,1)} %get-tuple-element.25), calls=%async_computation | async-start | bytes 2621440 | tf_op jit(solution)/shard_map/all_to_all | solution.py:476
  20.4 93.4 %all-gather.3.cloned.1.call-start = ((), (), s32[]{:S(2)}) async-start(), calls=%async_computation.1 | async-start | bytes 6963200 | tf_op jit(solution)/shard_map/all_gather | solution.py:478
  20.5 8.1 %collective-permute-start = (bf16[320,640]{1,0:T(8,128)(2,1)S(1)}, bf16[320,640]{1,0:T(8,128)(2,1)}, u32[]{:S(2)}, u32[]{:S(2)}) collective-permute-start(bf16[320,640]{1,0:T(8,128)(2,1)S(1)} %bitcast.33), channel_id=1, source_target_pairs={{1,24},{3,26},{5,28},{7,30},{9,16},{11,18},{13,20},{15,22},{16,9},... | collective-permute-start | bytes 1228808 | tf_op jit(solution)/shard_map/ppermute | solution.py:473
  47.5 44.3 %copy-start.5 = (s32[4]{0:T(128)S(1)}, s32[4]{0:T(128)}, u32[]{:S(2)}) copy-start(s32[4]{0:T(128)} %pad_add_fusion.place_ref) | copy-start | bytes 52
  47.5 44.3 %copy-start.6 = (s32[8,128]{1,0:T(8,128)S(1)}, s32[8,128]{1,0:T(8,128)}, u32[]{:S(2)}) copy-start(s32[8,128]{1,0:T(8,128)} %ids_ref.2) | copy-start | bytes 12292
  47.5 44.3 %copy-start.7 = (s32[8]{0:T(128)S(1)}, s32[8]{0:T(128)}, u32[]{:S(2)}) copy-start(s32[8]{0:T(128)} %lens_ref.5) | copy-start | bytes 100
  47.5 44.3 %copy-start.8 = (s32[16]{0:T(128)S(1)}, s32[16]{0:T(128)}, u32[]{:S(2)}) copy-start(s32[16]{0:T(128)} %get-tuple-element.23.info_ref) | copy-start | bytes 196
  47.6 11.0 %collective-permute-start.4 = (bf16[64,640]{1,0:T(8,128)(2,1)S(1)}, bf16[64,640]{1,0:T(8,128)(2,1)S(1)}, u32[]{:S(2)}, u32[]{:S(2)}) collective-permute-start(bf16[64,640]{1,0:T(8,128)(2,1)S(1)} %get-tuple-element.43), channel_id=1, source_target_pairs={{0,32},{8,40},{16,48},{24,56},{32,64},{40,72},{48,80},{56,88},{64,... | collective-permute-start | bytes 245768 | tf_op jit(solution)/shard_map/ppermute | solution.py:458
  47.7 13.6 %collective-permute-start.5 = (bf16[64,640]{1,0:T(8,128)(2,1)S(1)}, bf16[64,640]{1,0:T(8,128)(2,1)S(1)}, u32[]{:S(2)}, u32[]{:S(2)}) collective-permute-start(bf16[64,640]{1,0:T(8,128)(2,1)S(1)} %get-tuple-element.43), channel_id=1, source_target_pairs={{0,64},{8,72},{16,80},{24,88},{32,96},{40,104},{48,112},{56,120},{... | collective-permute-start | bytes 245768 | tf_op jit(solution)/shard_map/ppermute | solution.py:458
  49.5 11.7 %collective-permute-start.6 = (bf16[64,640]{1,0:T(8,128)(2,1)S(1)}, bf16[64,640]{1,0:T(8,128)(2,1)S(1)}, u32[]{:S(2)}, u32[]{:S(2)}) collective-permute-start(bf16[64,640]{1,0:T(8,128)(2,1)S(1)} %get-tuple-element.43), channel_id=1, source_target_pairs={{0,96},{8,104},{16,112},{24,120},{32,0},{40,8},{48,16},{56,24},{64... | collective-permute-start | bytes 245768 | tf_op jit(solution)/shard_map/ppermute | solution.py:458
  51.3 11.6 %collective-permute-start.1 = (bf16[64,640]{1,0:T(8,128)(2,1)S(1)}, bf16[64,640]{1,0:T(8,128)(2,1)S(1)}, u32[]{:S(2)}, u32[]{:S(2)}) collective-permute-start(bf16[64,640]{1,0:T(8,128)(2,1)S(1)} %get-tuple-element.44), channel_id=1, source_target_pairs={{0,8},{8,16},{16,24},{24,0},{32,40},{40,48},{48,56},{56,32},{64,72... | collective-permute-start | bytes 245768 | tf_op jit(solution)/shard_map/ppermute | solution.py:458
  51.3 13.8 %collective-permute-start.2 = (bf16[64,640]{1,0:T(8,128)(2,1)S(1)}, bf16[64,640]{1,0:T(8,128)(2,1)S(1)}, u32[]{:S(2)}, u32[]{:S(2)}) collective-permute-start(bf16[64,640]{1,0:T(8,128)(2,1)S(1)} %get-tuple-element.44), channel_id=1, source_target_pairs={{0,16},{8,24},{16,0},{24,8},{32,48},{40,56},{48,32},{56,40},{64,80... | collective-permute-start | bytes 245768 | tf_op jit(solution)/shard_map/ppermute | solution.py:458
  58.6 7.1 %collective-permute-start.3 = (bf16[64,640]{1,0:T(8,128)(2,1)S(1)}, bf16[64,640]{1,0:T(8,128)(2,1)S(1)}, u32[]{:S(2)}, u32[]{:S(2)}) collective-permute-start(bf16[64,640]{1,0:T(8,128)(2,1)S(1)} %get-tuple-element.44), channel_id=1, source_target_pairs={{0,24},{8,0},{16,8},{24,16},{32,56},{40,32},{48,40},{56,48},{64,88... | collective-permute-start | bytes 245768 | tf_op jit(solution)/shard_map/ppermute | solution.py:458
  65.8 11.4 %collective-permute-start.7 = (bf16[4,64,640]{2,1,0:T(8,128)(2,1)S(1)}, bf16[4,64,640]{2,1,0:T(8,128)(2,1)S(1)}, u32[]{:S(2)}, u32[]{:S(2)}) collective-permute-start(bf16[4,64,640]{2,1,0:T(8,128)(2,1)S(1)} %pad_maximum_fusion.refs_0_), channel_id=1, source_target_pairs={{0,32},{8,40},{16,48},{24,56},{32,64},{40,72},{48,80},{56,88},{64,... | collective-permute-start | bytes 983048 | tf_op jit(solution)/shard_map/ppermute | solution.py:458
  66.7 19.6 %collective-permute-start.10 = (bf16[4,64,640]{2,1,0:T(8,128)(2,1)S(1)}, bf16[4,64,640]{2,1,0:T(8,128)(2,1)S(1)}, u32[]{:S(2)}, u32[]{:S(2)}) collective-permute-start(bf16[4,64,640]{2,1,0:T(8,128)(2,1)S(1)} %pad_maximum_fusion.1.refs_4_), channel_id=1, source_target_pairs={{0,8},{8,16},{16,24},{24,0},{32,40},{40,48},{48,56},{56,32},{64,72... | collective-permute-start | bytes 983048 | tf_op jit(solution)/shard_map/ppermute | solution.py:458
  67.5 18.8 %collective-permute-start.11 = (bf16[4,64,640]{2,1,0:T(8,128)(2,1)S(1)}, bf16[4,64,640]{2,1,0:T(8,128)(2,1)S(1)}, u32[]{:S(2)}, u32[]{:S(2)}) collective-permute-start(bf16[4,64,640]{2,1,0:T(8,128)(2,1)S(1)} %pad_maximum_fusion.1.refs_4_), channel_id=1, source_target_pairs={{0,16},{8,24},{16,0},{24,8},{32,48},{40,56},{48,32},{56,40},{64,80... | collective-permute-start | bytes 983048 | tf_op jit(solution)/shard_map/ppermute | solution.py:458
  70.0 18.8 %collective-permute-start.12 = (bf16[4,64,640]{2,1,0:T(8,128)(2,1)S(1)}, bf16[4,64,640]{2,1,0:T(8,128)(2,1)S(1)}, u32[]{:S(2)}, u32[]{:S(2)}) collective-permute-start(bf16[4,64,640]{2,1,0:T(8,128)(2,1)S(1)} %pad_maximum_fusion.1.refs_4_), channel_id=1, source_target_pairs={{0,24},{8,0},{16,8},{24,16},{32,56},{40,32},{48,40},{56,48},{64,88... | collective-permute-start | bytes 983048 | tf_op jit(solution)/shard_map/ppermute | solution.py:458
  72.6 16.2 %collective-permute-start.8 = (bf16[4,64,640]{2,1,0:T(8,128)(2,1)S(1)}, bf16[4,64,640]{2,1,0:T(8,128)(2,1)S(1)}, u32[]{:S(2)}, u32[]{:S(2)}) collective-permute-start(bf16[4,64,640]{2,1,0:T(8,128)(2,1)S(1)} %pad_maximum_fusion.refs_0_), channel_id=1, source_target_pairs={{0,64},{8,72},{16,80},{24,88},{32,96},{40,104},{48,112},{56,120},{... | collective-permute-start | bytes 983048 | tf_op jit(solution)/shard_map/ppermute | solution.py:458
  77.2 14.6 %collective-permute-start.9 = (bf16[4,64,640]{2,1,0:T(8,128)(2,1)S(1)}, bf16[4,64,640]{2,1,0:T(8,128)(2,1)S(1)}, u32[]{:S(2)}, u32[]{:S(2)}) collective-permute-start(bf16[4,64,640]{2,1,0:T(8,128)(2,1)S(1)} %pad_maximum_fusion.refs_0_), channel_id=1, source_target_pairs={{0,96},{8,104},{16,112},{24,120},{32,0},{40,8},{48,16},{56,24},{64... | collective-permute-start | bytes 983048 | tf_op jit(solution)/shard_map/ppermute | solution.py:458
  96.1 3.1 %collective-permute-start.13 = (bf16[1024,640]{1,0:T(8,128)(2,1)S(1)}, bf16[1024,640]{1,0:T(8,128)(2,1)S(1)}, u32[]{:S(2)}, u32[]{:S(2)}) collective-permute-start(bf16[1024,640]{1,0:T(8,128)(2,1)S(1)} %attend.1.a_ref.a0.a1), channel_id=1, source_target_pairs={{0,1},{1,0},{2,3},{3,2},{4,5},{5,4},{6,7},{7,6},{8,9},{9,8},{10,11... | collective-permute-start | bytes 3932168 | tf_op jit(solution)/shard_map/ppermute | solution.py:494
  120.1 17.7 %collective-permute-start.14 = (bf16[512,640]{1,0:T(8,128)(2,1)S(1)}, bf16[512,640]{1,0:T(8,128)(2,1)S(1)}, u32[]{:S(2)}, u32[]{:S(2)}) collective-permute-start(bf16[512,640]{1,0:T(8,128)(2,1)S(1)} %get-tuple-element.35), channel_id=1, source_target_pairs={{0,2},{1,3},{2,4},{3,5},{4,6},{5,7},{6,0},{7,1},{8,10},{9,11},{10,... | collective-permute-start | bytes 1966088 | tf_op jit(solution)/shard_map/ppermute | solution.py:496
  121.7 17.6 %collective-permute-start.15 = (bf16[512,640]{1,0:T(8,128)(2,1)S(1)}, bf16[512,640]{1,0:T(8,128)(2,1)S(1)}, u32[]{:S(2)}, u32[]{:S(2)}) collective-permute-start(bf16[512,640]{1,0:T(8,128)(2,1)S(1)} %get-tuple-element.36), channel_id=1, source_target_pairs={{0,6},{1,7},{2,0},{3,1},{4,2},{5,3},{6,4},{7,5},{8,14},{9,15},{10,... | collective-permute-start | bytes 1966088 | tf_op jit(solution)/shard_map/ppermute | solution.py:497
  122.2 22.3 %slice-start.2 = ((s8[5242880]{0:T(1024)(128)(4,1)}), s8[4194304]{0:T(1024)(128)(4,1)S(1)}, s32[]{:S(2)}) async-start(s8[5242880]{0:T(1024)(128)(4,1)} %bitcast.31), calls=%async_computation.4 | async-start | bytes 8388608
  122.2 23.8 %slice-start = ((s8[6553600]{0:T(1024)(128)(4,1)}), s8[4194304]{0:T(1024)(128)(4,1)S(1)}, s32[]{:S(2)}) async-start(s8[6553600]{0:T(1024)(128)(4,1)} %bitcast.27), calls=%async_computation.2 | async-start | bytes 8388608
  125.3 26.5 %collective-permute-start.17 = (bf16[512,640]{1,0:T(8,128)(2,1)S(1)}, bf16[512,640]{1,0:T(8,128)(2,1)S(1)}, u32[]{:S(2)}, u32[]{:S(2)}) collective-permute-start(bf16[512,640]{1,0:T(8,128)(2,1)S(1)} %get-tuple-element.38), channel_id=1, source_target_pairs={{0,2},{1,3},{2,4},{3,5},{4,6},{5,7},{6,0},{7,1},{8,10},{9,11},{10,... | collective-permute-start | bytes 1966088 | tf_op jit(solution)/shard_map/ppermute | solution.py:499
  126.8 17.6 %slice-start.3 = ((s8[5242880]{0:T(1024)(128)(4,1)}), s8[1048576]{0:T(1024)(128)(4,1)S(1)}, s32[]{:S(2)}) async-start(s8[5242880]{0:T(1024)(128)(4,1)} %bitcast.31), calls=%async_computation.5 | async-start | bytes 2097152
  126.8 17.6 %copy-start.4 = (bf16[128,5120]{1,0:T(8,128)(2,1)S(1)}, bf16[128,5120]{1,0:T(8,128)(2,1)}, u32[]{:S(2)}) copy-start(bf16[128,5120]{1,0:T(8,128)(2,1)} %p_ref.5) | copy-start | bytes 3932164
  126.8 19.2 %slice-start.1 = ((s8[6553600]{0:T(1024)(128)(4,1)}), s8[2359296]{0:T(1024)(128)(4,1)S(1)}, s32[]{:S(2)}) async-start(s8[6553600]{0:T(1024)(128)(4,1)} %bitcast.27), calls=%async_computation.3 | async-start | bytes 4718592
  126.8 26.5 %collective-permute-start.18 = (bf16[512,640]{1,0:T(8,128)(2,1)S(1)}, bf16[512,640]{1,0:T(8,128)(2,1)S(1)}, u32[]{:S(2)}, u32[]{:S(2)}) collective-permute-start(bf16[512,640]{1,0:T(8,128)(2,1)S(1)} %get-tuple-element.39), channel_id=1, source_target_pairs={{0,6},{1,7},{2,0},{3,1},{4,2},{5,3},{6,4},{7,5},{8,14},{9,15},{10,... | collective-permute-start | bytes 1966088 | tf_op jit(solution)/shard_map/ppermute | solution.py:500
  142.4 22.6 %collective-permute-start.16 = (bf16[512,640]{1,0:T(8,128)(2,1)S(1)}, bf16[512,640]{1,0:T(8,128)(2,1)S(1)}, u32[]{:S(2)}, u32[]{:S(2)}) collective-permute-start(bf16[512,640]{1,0:T(8,128)(2,1)S(1)} %get-tuple-element.37), channel_id=1, source_target_pairs={{0,2},{1,3},{2,4},{3,5},{4,6},{5,7},{6,0},{7,1},{8,10},{9,11},{10,... | collective-permute-start | bytes 1966088 | tf_op jit(solution)/shard_map/ppermute | solution.py:502
  143.6 22.5 %collective-permute-start.19 = (bf16[512,640]{1,0:T(8,128)(2,1)S(1)}, bf16[512,640]{1,0:T(8,128)(2,1)S(1)}, u32[]{:S(2)}, u32[]{:S(2)}) collective-permute-start(bf16[512,640]{1,0:T(8,128)(2,1)S(1)} %get-tuple-element.40), channel_id=1, source_target_pairs={{0,6},{1,7},{2,0},{3,1},{4,2},{5,3},{6,4},{7,5},{8,14},{9,15},{10,... | collective-permute-start | bytes 1966088 | tf_op jit(solution)/shard_map/ppermute | solution.py:503
  (4 other events, 15.9 us)
Sparse Core Ops, SparseCore 0:
  41.1 72.6 all-gather.2

commit v3 on v2

--- a/solution.py
+++ b/solution.py
@@ -43,7 +43,8 @@
         groups = (lens_ref[s] + GROUP - 1) // GROUP
         total = total + jnp.where(s < live, groups, 0)
     info_ref[SLOTS] = live
-    line = jnp.broadcast_to(gain_ref[pl.ds(row // 2, 1), :], (8, 2 * BLOCK))
+    begin = pl.multiple_of((row // 2) * 2 * BLOCK, 2 * BLOCK)
+    line = jnp.broadcast_to(gain_ref[:, pl.ds(begin, 2 * BLOCK)], (8, 2 * BLOCK))
     turned_ref[...] = line.T
     start = pl.multiple_of((row % 2) * BLOCK, 8)
     gain = turned_ref[pl.ds(start, BLOCK), :][:, :1]
@@ -62,7 +63,7 @@
         grid_spec=pltpu.PrefetchScalarGridSpec(
             num_scalar_prefetch=3,
             grid=(1,),
-            in_specs=[pl.BlockSpec((8, 2 * BLOCK), lambda i, *_: (0, 0)), stay, stay, stay],
+            in_specs=[pl.BlockSpec((1, D), lambda i, *_: (0, 0)), stay, stay, stay],
             out_specs=[
                 pl.BlockSpec((ROWS, BLOCK, DH), lambda i, *_: (0, 0, 0)),
                 pl.BlockSpec(memory_space=pltpu.SMEM),
@@ -459,7 +460,7 @@
         return [value, near[1], near[2], near[3]]
 
     packed, info = pack(
-        place, set_lengths, live_counts, norm_gain.reshape(8, 2 * BLOCK), w_query, w_key, w_value
+        place, set_lengths, live_counts, norm_gain.reshape(1, D), w_query, w_key, w_value
     )
     packed, w_out, embed_late = lax.optimization_barrier((packed, w_out, embed_table))
     turned = w_out.T

time: 177 us -> 176 us (level)
  Pallas kernels: 34.2 us -> 38 us
  waiting for transfers between devices: 80.8 us -> 77.1 us
    all_gather x1, waiting for transfers between devices: 14.6 us -> 9.66 us  [on_device(): w_all = lax.all_gather(tiles, 'row', axis=0)]
    pallas_call x1, Pallas kernels: 4.22 us -> 7.42 us  [attend(): pl.pallas_call(attend_kernel, grid_spec=pltpu.PrefetchScalarGridSpec(num_...]
  transfers between devices with their start and end apart: 22 -> 22, of which waited for: 16 -> 16; matrix products, arithmetic and copies ran while one was open for 1% -> 1% of each run, Pallas kernels for 13% -> 15%
where the time goes in v3:
time: 176 us; the launch traced here: 175 us
  waiting for transfers between devices  77.1 us (44%)
  Pallas kernels  38 us (22%)
  starting transfers between devices  37.1 us (21%)
  between operations  13.6 us (8%)
  local copies, waits for them, and re-layouts  7.91 us (4%)
    ppermute x12, waiting for transfers between devices, spread(): lax.ppermute(value, 'row', shifted(o, along_x))  24.6 us
    ppermute x12, starting transfers between devices, spread(): lax.ppermute(value, 'row', shifted(o, along_x))  21.3 us
    all_to_all x1, waiting for transfers between devices, on_device(): w_block = lax.all_to_all(packed, 'row', 0, 0)  11.6 us
    ppermute x1, waiting for transfers between devices, rest(): below_high = lax.ppermute(up, 'mp', along(1))  11.6 us
    ppermute x1, waiting for transfers between devices, rest(): from_below = lax.ppermute(top, 'mp', along(1))  10.4 us
    all_gather x1, waiting for transfers between devices, on_device(): w_all = lax.all_gather(tiles, 'row', axis=0)  9.66 us
    all_to_all x1, starting transfers between devices, on_device(): w_block = lax.all_to_all(packed, 'row', 0, 0)  8.02 us
    unnamed x28, local copies, waits for them, and re-layouts  7.88 us
  transfers between devices with their start and end apart: 22, of which 16 were waited for; matrix products, arithmetic and copies ran while one was open for 1% of the time, Pallas kernels for 15%

profile of v3, /device:TPU:8, one launch (start us, length us, event | category | flops | bytes accessed | tf_op | source)
XLA Modules:
  0.0 175.3 jit_solution(9474403259131208279)
XLA Ops:
  7.2 3.9 %pack.1 = (bf16[16,320,128]{2,1,0:T(8,128)(2,1)}, s32[16]{0:T(128)}) custom-call(s32[4]{0:T(128)} %pad_add_fusion.place_ref, s32[8]{0:T(128)} %lens_ref.5, s32[16]{0:T(128)} %counts_ref.1, f32[1,5120]{1,0:T(1,128)} %bitcast.41, bf16[320,640]{1,0:T(8,128)(2,1)} %q_hbm.1, bf16[320,640]{1,0:T(8,128)(2,1)} %k_hbm.1, bf16[320,640]{1,0:T(8,128)(2,1)} %v_hbm.1), custom_call_target="tpu_custom_call" | custom-call | tf_op jit(solution)/shard_map/pack/pallas_call | solution.py:61
  11.0 8.0 %all-to-all-start = ((bf16[16,320,128]{2,1,0:T(8,128)(2,1)}), bf16[16,320,128]{2,1,0:T(8,128)(2,1)S(1)}, u32[]{:S(2)}, u32[]{:S(2)}) async-start(bf16[16,320,128]{2,1,0:T(8,128)(2,1)} %get-tuple-element.25), calls=%async_computation | async-start | bytes 2621440 | tf_op jit(solution)/shard_map/all_to_all | solution.py:477
  20.5 2.5 %copy-done.1 = bf16[512,5120]{1,0:T(8,128)(2,1)S(1)} copy-done((bf16[512,5120]{1,0:T(8,128)(2,1)S(1)}, bf16[512,5120]{1,0:T(8,128)(2,1)}, u32[]{:S(2)}) %copy-start.1) | copy-done | bytes 5242904
  23.0 4.2 %norm_scales.1.r_ref = f32[512,128]{1,0:T(8,128)S(1)} custom-call(bf16[512,5120]{1,0:T(8,128)(2,1)S(1)} %copy-done.1, bf16[128,5120]{1,0:T(8,128)(2,1)S(1)} %copy-done.3), custom_call_target="tpu_custom_call" | custom-call | flops 838860800 | bytes 6553600 | tf_op jit(solution)/shard_map/norm_scales/pallas_call | solution.py:150
  28.0 11.6 %all-to-all-done.w_ref = bf16[16,320,128]{2,1,0:T(8,128)(2,1)S(1)} async-done(((bf16[16,320,128]{2,1,0:T(8,128)(2,1)}), bf16[16,320,128]{2,1,0:T(8,128)(2,1)S(1)}, u32[]{:S(2)}, u32[]{:S(2)}) %all-to-all-start) | async-done | bytes 1310752 | tf_op jit(solution)/shard_map/all_to_all | solution.py:477
  39.7 2.5 %copy-done.2 = bf16[512,5120]{1,0:T(8,128)(2,1)S(1)} copy-done((bf16[512,5120]{1,0:T(8,128)(2,1)S(1)}, bf16[512,5120]{1,0:T(8,128)(2,1)}, u32[]{:S(2)}) %copy-start.2) | copy-done | bytes 5242904
  42.1 4.0 %project_tables.1 = bf16[128,640]{1,0:T(8,128)(2,1)S(1)} custom-call(bf16[512,5120]{1,0:T(8,128)(2,1)S(1)} %copy-done.2, bf16[128,5120]{1,0:T(8,128)(2,1)S(1)} %copy-done.3, bf16[16,320,128]{2,1,0:T(8,128)(2,1)S(1)} %all-to-all-done.w_ref), custom_call_target="tpu_custom_call" | custom-call | tf_op jit(solution)/shard_map/project_tables/pallas_call | solution.py:103
  46.4 1.8 %collective-permute-start.5 = (bf16[64,640]{1,0:T(8,128)(2,1)S(1)}, bf16[64,640]{1,0:T(8,128)(2,1)S(1)}, u32[]{:S(2)}, u32[]{:S(2)}) collective-permute-start(bf16[64,640]{1,0:T(8,128)(2,1)S(1)} %get-tuple-element.43), channel_id=1, source_target_pairs={{0,64},{8,72},{16,80},{24,88},{32,96},{40,104},{48,112},{56,120},{... | collective-permute-start | bytes 245768 | tf_op jit(solution)/shard_map/ppermute | solution.py:459
  48.2 1.8 %collective-permute-start.6 = (bf16[64,640]{1,0:T(8,128)(2,1)S(1)}, bf16[64,640]{1,0:T(8,128)(2,1)S(1)}, u32[]{:S(2)}, u32[]{:S(2)}) collective-permute-start(bf16[64,640]{1,0:T(8,128)(2,1)S(1)} %get-tuple-element.43), channel_id=1, source_target_pairs={{0,96},{8,104},{16,112},{24,120},{32,0},{40,8},{48,16},{56,24},{64... | collective-permute-start | bytes 245768 | tf_op jit(solution)/shard_map/ppermute | solution.py:459
  50.0 7.3 %collective-permute-start.2 = (bf16[64,640]{1,0:T(8,128)(2,1)S(1)}, bf16[64,640]{1,0:T(8,128)(2,1)S(1)}, u32[]{:S(2)}, u32[]{:S(2)}) collective-permute-start(bf16[64,640]{1,0:T(8,128)(2,1)S(1)} %get-tuple-element.44), channel_id=1, source_target_pairs={{0,16},{8,24},{16,0},{24,8},{32,48},{40,56},{48,32},{56,40},{64,80... | collective-permute-start | bytes 245768 | tf_op jit(solution)/shard_map/ppermute | solution.py:459
  57.3 2.6 %collective-permute-start.3 = (bf16[64,640]{1,0:T(8,128)(2,1)S(1)}, bf16[64,640]{1,0:T(8,128)(2,1)S(1)}, u32[]{:S(2)}, u32[]{:S(2)}) collective-permute-start(bf16[64,640]{1,0:T(8,128)(2,1)S(1)} %get-tuple-element.44), channel_id=1, source_target_pairs={{0,24},{8,0},{16,8},{24,16},{32,56},{40,32},{48,40},{56,48},{64,88... | collective-permute-start | bytes 245768 | tf_op jit(solution)/shard_map/ppermute | solution.py:459
  61.5 2.2 %collective-permute-done.2 = bf16[64,640]{1,0:T(8,128)(2,1)S(1)} collective-permute-done((bf16[64,640]{1,0:T(8,128)(2,1)S(1)}, bf16[64,640]{1,0:T(8,128)(2,1)S(1)}, u32[]{:S(2)}, u32[]{:S(2)}) %collective-permute-start.2) | collective-permute-done | bytes 81952 | tf_op jit(solution)/shard_map/ppermute | solution.py:459
  66.2 2.5 %collective-permute-start.11 = (bf16[4,64,640]{2,1,0:T(8,128)(2,1)S(1)}, bf16[4,64,640]{2,1,0:T(8,128)(2,1)S(1)}, u32[]{:S(2)}, u32[]{:S(2)}) collective-permute-start(bf16[4,64,640]{2,1,0:T(8,128)(2,1)S(1)} %pad_maximum_fusion.1.refs_4_), channel_id=1, source_target_pairs={{0,16},{8,24},{16,0},{24,8},{32,48},{40,56},{48,32},{56,40},{64,80... | collective-permute-start | bytes 983048 | tf_op jit(solution)/shard_map/ppermute | solution.py:459
  68.7 2.6 %collective-permute-start.12 = (bf16[4,64,640]{2,1,0:T(8,128)(2,1)S(1)}, bf16[4,64,640]{2,1,0:T(8,128)(2,1)S(1)}, u32[]{:S(2)}, u32[]{:S(2)}) collective-permute-start(bf16[4,64,640]{2,1,0:T(8,128)(2,1)S(1)} %pad_maximum_fusion.1.refs_4_), channel_id=1, source_target_pairs={{0,24},{8,0},{16,8},{24,16},{32,56},{40,32},{48,40},{56,48},{64,88... | collective-permute-start | bytes 983048 | tf_op jit(solution)/shard_map/ppermute | solution.py:459
  71.3 4.6 %collective-permute-done.7.refs_1_ = bf16[4,64,640]{2,1,0:T(8,128)(2,1)S(1)} collective-permute-done((bf16[4,64,640]{2,1,0:T(8,128)(2,1)S(1)}, bf16[4,64,640]{2,1,0:T(8,128)(2,1)S(1)}, u32[]{:S(2)}, u32[]{:S(2)}) %collective-permute-start.7) | collective-permute-done | bytes 327712 | tf_op jit(solution)/shard_map/ppermute | solution.py:459
  76.7 9.1 %collective-permute-done.10.refs_5_ = bf16[4,64,640]{2,1,0:T(8,128)(2,1)S(1)} collective-permute-done((bf16[4,64,640]{2,1,0:T(8,128)(2,1)S(1)}, bf16[4,64,640]{2,1,0:T(8,128)(2,1)S(1)}, u32[]{:S(2)}, u32[]{:S(2)}) %collective-permute-start.10) | collective-permute-done | bytes 327712 | tf_op jit(solution)/shard_map/ppermute | solution.py:459
  85.7 3.4 %collective-permute-done.12.refs_7_ = bf16[4,64,640]{2,1,0:T(8,128)(2,1)S(1)} collective-permute-done((bf16[4,64,640]{2,1,0:T(8,128)(2,1)S(1)}, bf16[4,64,640]{2,1,0:T(8,128)(2,1)S(1)}, u32[]{:S(2)}, u32[]{:S(2)}) %collective-permute-start.12) | collective-permute-done | bytes 327712 | tf_op jit(solution)/shard_map/ppermute | solution.py:459
  89.1 3.1 %collective-permute-done.9.refs_3_ = bf16[4,64,640]{2,1,0:T(8,128)(2,1)S(1)} collective-permute-done((bf16[4,64,640]{2,1,0:T(8,128)(2,1)S(1)}, bf16[4,64,640]{2,1,0:T(8,128)(2,1)S(1)}, u32[]{:S(2)}, u32[]{:S(2)}) %collective-permute-start.9) | collective-permute-done | bytes 327712 | tf_op jit(solution)/shard_map/ppermute | solution.py:459
  92.3 7.4 %attend.1.a_ref.a0.a1 = bf16[1024,640]{1,0:T(8,128)(2,1)S(1)} custom-call(s32[8]{0:T(128)S(1)} %copy-done.7, s32[16]{0:T(128)S(1)} %copy-done.8, s32[4]{0:T(128)S(1)} %copy-done.5, s32[8,128]{1,0:T(8,128)S(1)} %copy-done.6, f32[512,128]{1,0:T(8,128)S(1)} %norm_scales.1.r_ref, bf16[4,64,640]{2,1,0:T(8,128)(2,1)S(1)} %pad_maximum_fusion.refs_0_, ...), custom_call_target="tpu_custom_call" | custom-call | tf_op jit(solution)/shard_map/attend/pallas_call | solution.py:260
  99.8 3.0 %collective-permute-done.13.other_ref.o0.o1 = bf16[1024,640]{1,0:T(8,128)(2,1)S(1)} collective-permute-done((bf16[1024,640]{1,0:T(8,128)(2,1)S(1)}, bf16[1024,640]{1,0:T(8,128)(2,1)S(1)}, u32[]{:S(2)}, u32[]{:S(2)}) %collective-permute-start.13) | collective-permute-done | bytes 1310752 | tf_op jit(solution)/shard_map/ppermute | solution.py:495
  102.8 9.7 %all-gather.3.cloned.1.call-done = bf16[5120,640]{1,0:T(8,128)(2,1)} async-done(((bf16[320,640]{1,0:T(8,128)(2,1)}), bf16[5120,640]{1,0:T(8,128)(2,1)}) %all-gather.3.cloned.1.call-update) | async-done | bytes 6553616 | tf_op jit(solution)/shard_map/all_gather | solution.py:479
  112.5 2.9 %copy-done = bf16[5120,640]{1,0:T(8,128)(2,1)S(1)} copy-done((bf16[5120,640]{1,0:T(8,128)(2,1)S(1)}, bf16[5120,640]{1,0:T(8,128)(2,1)}, u32[]{:S(2)}) %copy-start) | copy-done | bytes 6553624
  115.3 3.4 %far_partials.1 = (bf16[512,640]{1,0:T(8,128)(2,1)S(1)}, bf16[512,640]{1,0:T(8,128)(2,1)S(1)}) custom-call(s32[4]{0:T(128)S(1)} %copy-done.5, bf16[1024,640]{1,0:T(8,128)(2,1)S(1)} %attend.1.a_ref.a0.a1, bf16[1024,640]{1,0:T(8,128)(2,1)S(1)} %collective-permute-done.13.other_ref.o0.o1, bf16[16,320,640]{2,1,0:T(8,128)(2,1)S(1)} %bitcast.18, ...), custom_call_target="tpu_custom_call" | custom-call | tf_op jit(solution)/shard_map/far_partials/pallas_call | solution.py:315
  120.9 3.1 %free_partials.1 = (bf16[512,640]{1,0:T(8,128)(2,1)S(1)}, bf16[512,640]{1,0:T(8,128)(2,1)S(1)}) custom-call(s32[4]{0:T(128)S(1)} %copy-done.5, bf16[1024,640]{1,0:T(8,128)(2,1)S(1)} %attend.1.a_ref.a0.a1, bf16[1024,640]{1,0:T(8,128)(2,1)S(1)} %collective-permute-done.13.other_ref.o0.o1, bf16[1024,640]{1,0:T(8,128)(2,1)S(1)} %attend.1.a_ref.a0.a1, ...), custom_call_target="tpu_custom_call" | custom-call | tf_op jit(solution)/shard_map/free_partials/pallas_call | solution.py:338
  123.9 1.6 collective-permute-start.17
  126.0 10.4 %collective-permute-done.14.from_below = bf16[512,640]{1,0:T(8,128)(2,1)S(1)} collective-permute-done((bf16[512,640]{1,0:T(8,128)(2,1)S(1)}, bf16[512,640]{1,0:T(8,128)(2,1)S(1)}, u32[]{:S(2)}, u32[]{:S(2)}) %collective-permute-start.14) | collective-permute-done | bytes 655392 | tf_op jit(solution)/shard_map/ppermute | solution.py:497
  138.0 3.1 %relay_partials.1 = (bf16[512,640]{1,0:T(8,128)(2,1)S(1)}, bf16[512,640]{1,0:T(8,128)(2,1)S(1)}) custom-call(s32[4]{0:T(128)S(1)} %copy-done.5, bf16[1024,640]{1,0:T(8,128)(2,1)S(1)} %attend.1.a_ref.a0.a1, bf16[1024,640]{1,0:T(8,128)(2,1)S(1)} %collective-permute-done.13.other_ref.o0.o1, bf16[1024,640]{1,0:T(8,128)(2,1)S(1)} %attend.1.a_ref.a0.a1, ...), custom_call_target="tpu_custom_call" | custom-call | tf_op jit(solution)/shard_map/relay_partials/pallas_call | solution.py:361
  143.1 2.1 %residual.1.stored_ref = bf16[8,128,640]{2,1,0:T(8,128)(2,1)S(1)} custom-call(s32[16]{0:T(128)S(1)} %copy-done.8, s32[4]{0:T(128)S(1)} %copy-done.5, s32[8,128]{1,0:T(8,128)S(1)} %copy-done.6, bf16[512,5120]{1,0:T(8,128)(2,1)S(1)} %bitcast.33, bf16[128,5120]{1,0:T(8,128)(2,1)S(1)} %copy-done.4), custom_call_target="tpu_custom_call" | custom-call | flops 671088640 | bytes 2621440 | tf_op jit(solution)/shard_map/residual/pallas_call | solution.py:186
  145.3 3.3 %base_partial.1.base_ref = f32[1024,640]{1,0:T(8,128)S(1)} custom-call(s32[4]{0:T(128)S(1)} %copy-done.5, bf16[1024,640]{1,0:T(8,128)(2,1)S(1)} %attend.1.a_ref.a0.a1, bf16[1024,640]{1,0:T(8,128)(2,1)S(1)} %collective-permute-done.13.other_ref.o0.o1, bf16[16,320,640]{2,1,0:T(8,128)(2,1)S(1)} %bitcast.30, bf16[16,320,640]{2,1,0:T(8,128)(2,1)S(1)} %bitcast.31), custom_call_target="tpu_custom_call" | custom-call | tf_op jit(solution)/shard_map/base_partial/pallas_call | solution.py:382
  148.6 1.9 %collective-permute-done.17.refs_1_ = bf16[512,640]{1,0:T(8,128)(2,1)S(1)} collective-permute-done((bf16[512,640]{1,0:T(8,128)(2,1)S(1)}, bf16[512,640]{1,0:T(8,128)(2,1)S(1)}, u32[]{:S(2)}, u32[]{:S(2)}) %collective-permute-start.17) | collective-permute-done | bytes 655392 | tf_op jit(solution)/shard_map/ppermute | solution.py:500
  152.0 11.6 %collective-permute-done.16.refs_0_ = bf16[512,640]{1,0:T(8,128)(2,1)S(1)} collective-permute-done((bf16[512,640]{1,0:T(8,128)(2,1)S(1)}, bf16[512,640]{1,0:T(8,128)(2,1)S(1)}, u32[]{:S(2)}, u32[]{:S(2)}) %collective-permute-start.16) | collective-permute-done | bytes 655392 | tf_op jit(solution)/shard_map/ppermute | solution.py:503
  164.8 3.6 %finish.1 = bf16[8,128,640]{2,1,0:T(8,128)(2,1)} custom-call(s32[8]{0:T(128)S(1)} %copy-done.7, s32[16]{0:T(128)S(1)} %copy-done.8, bf16[8,128,640]{2,1,0:T(8,128)(2,1)S(1)} %residual.1.stored_ref, f32[1024,640]{1,0:T(8,128)S(1)} %base_partial.1.base_ref, bf16[512,640]{1,0:T(8,128)(2,1)S(1)} %collective-permute-done.16.refs_0_, ...), custom_call_target="tpu_custom_call" | custom-call | tf_op jit(solution)/shard_map/finish/pallas_call | solution.py:419
  (58 shorter events, 17.0 us)
Async XLA Ops:
  11.0 9.5 %copy-start.3 = (bf16[128,5120]{1,0:T(8,128)(2,1)S(1)}, bf16[128,5120]{1,0:T(8,128)(2,1)}, u32[]{:S(2)}) copy-start(bf16[128,5120]{1,0:T(8,128)(2,1)} %p_ref.5) | copy-start | bytes 3932164
  11.0 28.6 %all-to-all-start = ((bf16[16,320,128]{2,1,0:T(8,128)(2,1)}), bf16[16,320,128]{2,1,0:T(8,128)(2,1)S(1)}, u32[]{:S(2)}, u32[]{:S(2)}) async-start(bf16[16,320,128]{2,1,0:T(8,128)(2,1)} %get-tuple-element.25), calls=%async_computation | async-start | bytes 2621440 | tf_op jit(solution)/shard_map/all_to_all | solution.py:477
  19.1 93.4 %all-gather.3.cloned.1.call-start = ((), (), s32[]{:S(2)}) async-start(), calls=%async_computation.1 | async-start | bytes 6963200 | tf_op jit(solution)/shard_map/all_gather | solution.py:479
  19.1 8.1 %collective-permute-start = (bf16[320,640]{1,0:T(8,128)(2,1)S(1)}, bf16[320,640]{1,0:T(8,128)(2,1)}, u32[]{:S(2)}, u32[]{:S(2)}) collective-permute-start(bf16[320,640]{1,0:T(8,128)(2,1)S(1)} %bitcast.34), channel_id=1, source_target_pairs={{1,24},{3,26},{5,28},{7,30},{9,16},{11,18},{13,20},{15,22},{16,9},... | collective-permute-start | bytes 1228808 | tf_op jit(solution)/shard_map/ppermute | solution.py:474
  46.2 46.1 %copy-start.5 = (s32[4]{0:T(128)S(1)}, s32[4]{0:T(128)}, u32[]{:S(2)}) copy-start(s32[4]{0:T(128)} %pad_add_fusion.place_ref) | copy-start | bytes 52
  46.2 46.1 %copy-start.6 = (s32[8,128]{1,0:T(8,128)S(1)}, s32[8,128]{1,0:T(8,128)}, u32[]{:S(2)}) copy-start(s32[8,128]{1,0:T(8,128)} %ids_ref.2) | copy-start | bytes 12292
  46.2 46.1 %copy-start.7 = (s32[8]{0:T(128)S(1)}, s32[8]{0:T(128)}, u32[]{:S(2)}) copy-start(s32[8]{0:T(128)} %lens_ref.5) | copy-start | bytes 100
  46.2 46.0 %copy-start.8 = (s32[16]{0:T(128)S(1)}, s32[16]{0:T(128)}, u32[]{:S(2)}) copy-start(s32[16]{0:T(128)} %get-tuple-element.23.info_ref) | copy-start | bytes 196
  46.3 11.0 %collective-permute-start.4 = (bf16[64,640]{1,0:T(8,128)(2,1)S(1)}, bf16[64,640]{1,0:T(8,128)(2,1)S(1)}, u32[]{:S(2)}, u32[]{:S(2)}) collective-permute-start(bf16[64,640]{1,0:T(8,128)(2,1)S(1)} %get-tuple-element.43), channel_id=1, source_target_pairs={{0,32},{8,40},{16,48},{24,56},{32,64},{40,72},{48,80},{56,88},{64,... | collective-permute-start | bytes 245768 | tf_op jit(solution)/shard_map/ppermute | solution.py:459
  46.4 13.6 %collective-permute-start.5 = (bf16[64,640]{1,0:T(8,128)(2,1)S(1)}, bf16[64,640]{1,0:T(8,128)(2,1)S(1)}, u32[]{:S(2)}, u32[]{:S(2)}) collective-permute-start(bf16[64,640]{1,0:T(8,128)(2,1)S(1)} %get-tuple-element.43), channel_id=1, source_target_pairs={{0,64},{8,72},{16,80},{24,88},{32,96},{40,104},{48,112},{56,120},{... | collective-permute-start | bytes 245768 | tf_op jit(solution)/shard_map/ppermute | solution.py:459
  48.2 11.7 %collective-permute-start.6 = (bf16[64,640]{1,0:T(8,128)(2,1)S(1)}, bf16[64,640]{1,0:T(8,128)(2,1)S(1)}, u32[]{:S(2)}, u32[]{:S(2)}) collective-permute-start(bf16[64,640]{1,0:T(8,128)(2,1)S(1)} %get-tuple-element.43), channel_id=1, source_target_pairs={{0,96},{8,104},{16,112},{24,120},{32,0},{40,8},{48,16},{56,24},{64... | collective-permute-start | bytes 245768 | tf_op jit(solution)/shard_map/ppermute | solution.py:459
  50.0 11.6 %collective-permute-start.1 = (bf16[64,640]{1,0:T(8,128)(2,1)S(1)}, bf16[64,640]{1,0:T(8,128)(2,1)S(1)}, u32[]{:S(2)}, u32[]{:S(2)}) collective-permute-start(bf16[64,640]{1,0:T(8,128)(2,1)S(1)} %get-tuple-element.44), channel_id=1, source_target_pairs={{0,8},{8,16},{16,24},{24,0},{32,40},{40,48},{48,56},{56,32},{64,72... | collective-permute-start | bytes 245768 | tf_op jit(solution)/shard_map/ppermute | solution.py:459
  50.0 13.8 %collective-permute-start.2 = (bf16[64,640]{1,0:T(8,128)(2,1)S(1)}, bf16[64,640]{1,0:T(8,128)(2,1)S(1)}, u32[]{:S(2)}, u32[]{:S(2)}) collective-permute-start(bf16[64,640]{1,0:T(8,128)(2,1)S(1)} %get-tuple-element.44), channel_id=1, source_target_pairs={{0,16},{8,24},{16,0},{24,8},{32,48},{40,56},{48,32},{56,40},{64,80... | collective-permute-start | bytes 245768 | tf_op jit(solution)/shard_map/ppermute | solution.py:459
  57.3 7.1 %collective-permute-start.3 = (bf16[64,640]{1,0:T(8,128)(2,1)S(1)}, bf16[64,640]{1,0:T(8,128)(2,1)S(1)}, u32[]{:S(2)}, u32[]{:S(2)}) collective-permute-start(bf16[64,640]{1,0:T(8,128)(2,1)S(1)} %get-tuple-element.44), channel_id=1, source_target_pairs={{0,24},{8,0},{16,8},{24,16},{32,56},{40,32},{48,40},{56,48},{64,88... | collective-permute-start | bytes 245768 | tf_op jit(solution)/shard_map/ppermute | solution.py:459
  64.5 11.4 %collective-permute-start.7 = (bf16[4,64,640]{2,1,0:T(8,128)(2,1)S(1)}, bf16[4,64,640]{2,1,0:T(8,128)(2,1)S(1)}, u32[]{:S(2)}, u32[]{:S(2)}) collective-permute-start(bf16[4,64,640]{2,1,0:T(8,128)(2,1)S(1)} %pad_maximum_fusion.refs_0_), channel_id=1, source_target_pairs={{0,32},{8,40},{16,48},{24,56},{32,64},{40,72},{48,80},{56,88},{64,... | collective-permute-start | bytes 983048 | tf_op jit(solution)/shard_map/ppermute | solution.py:459
  65.4 20.4 %collective-permute-start.10 = (bf16[4,64,640]{2,1,0:T(8,128)(2,1)S(1)}, bf16[4,64,640]{2,1,0:T(8,128)(2,1)S(1)}, u32[]{:S(2)}, u32[]{:S(2)}) collective-permute-start(bf16[4,64,640]{2,1,0:T(8,128)(2,1)S(1)} %pad_maximum_fusion.1.refs_4_), channel_id=1, source_target_pairs={{0,8},{8,16},{16,24},{24,0},{32,40},{40,48},{48,56},{56,32},{64,72... | collective-permute-start | bytes 983048 | tf_op jit(solution)/shard_map/ppermute | solution.py:459
  66.2 19.5 %collective-permute-start.11 = (bf16[4,64,640]{2,1,0:T(8,128)(2,1)S(1)}, bf16[4,64,640]{2,1,0:T(8,128)(2,1)S(1)}, u32[]{:S(2)}, u32[]{:S(2)}) collective-permute-start(bf16[4,64,640]{2,1,0:T(8,128)(2,1)S(1)} %pad_maximum_fusion.1.refs_4_), channel_id=1, source_target_pairs={{0,16},{8,24},{16,0},{24,8},{32,48},{40,56},{48,32},{56,40},{64,80... | collective-permute-start | bytes 983048 | tf_op jit(solution)/shard_map/ppermute | solution.py:459
  68.7 20.5 %collective-permute-start.12 = (bf16[4,64,640]{2,1,0:T(8,128)(2,1)S(1)}, bf16[4,64,640]{2,1,0:T(8,128)(2,1)S(1)}, u32[]{:S(2)}, u32[]{:S(2)}) collective-permute-start(bf16[4,64,640]{2,1,0:T(8,128)(2,1)S(1)} %pad_maximum_fusion.1.refs_4_), channel_id=1, source_target_pairs={{0,24},{8,0},{16,8},{24,16},{32,56},{40,32},{48,40},{56,48},{64,88... | collective-permute-start | bytes 983048 | tf_op jit(solution)/shard_map/ppermute | solution.py:459
  71.3 17.8 %collective-permute-start.8 = (bf16[4,64,640]{2,1,0:T(8,128)(2,1)S(1)}, bf16[4,64,640]{2,1,0:T(8,128)(2,1)S(1)}, u32[]{:S(2)}, u32[]{:S(2)}) collective-permute-start(bf16[4,64,640]{2,1,0:T(8,128)(2,1)S(1)} %pad_maximum_fusion.refs_0_), channel_id=1, source_target_pairs={{0,64},{8,72},{16,80},{24,88},{32,96},{40,104},{48,112},{56,120},{... | collective-permute-start | bytes 983048 | tf_op jit(solution)/shard_map/ppermute | solution.py:459
  75.9 16.4 %collective-permute-start.9 = (bf16[4,64,640]{2,1,0:T(8,128)(2,1)S(1)}, bf16[4,64,640]{2,1,0:T(8,128)(2,1)S(1)}, u32[]{:S(2)}, u32[]{:S(2)}) collective-permute-start(bf16[4,64,640]{2,1,0:T(8,128)(2,1)S(1)} %pad_maximum_fusion.refs_0_), channel_id=1, source_target_pairs={{0,96},{8,104},{16,112},{24,120},{32,0},{40,8},{48,16},{56,24},{64... | collective-permute-start | bytes 983048 | tf_op jit(solution)/shard_map/ppermute | solution.py:459
  99.7 3.1 %collective-permute-start.13 = (bf16[1024,640]{1,0:T(8,128)(2,1)S(1)}, bf16[1024,640]{1,0:T(8,128)(2,1)S(1)}, u32[]{:S(2)}, u32[]{:S(2)}) collective-permute-start(bf16[1024,640]{1,0:T(8,128)(2,1)S(1)} %attend.1.a_ref.a0.a1), channel_id=1, source_target_pairs={{0,1},{1,0},{2,3},{3,2},{4,5},{5,4},{6,7},{7,6},{8,9},{9,8},{10,11... | collective-permute-start | bytes 3932168 | tf_op jit(solution)/shard_map/ppermute | solution.py:495
  118.8 17.7 %collective-permute-start.14 = (bf16[512,640]{1,0:T(8,128)(2,1)S(1)}, bf16[512,640]{1,0:T(8,128)(2,1)S(1)}, u32[]{:S(2)}, u32[]{:S(2)}) collective-permute-start(bf16[512,640]{1,0:T(8,128)(2,1)S(1)} %get-tuple-element.35), channel_id=1, source_target_pairs={{0,2},{1,3},{2,4},{3,5},{4,6},{5,7},{6,0},{7,1},{8,10},{9,11},{10,... | collective-permute-start | bytes 1966088 | tf_op jit(solution)/shard_map/ppermute | solution.py:497
  120.3 17.6 %collective-permute-start.15 = (bf16[512,640]{1,0:T(8,128)(2,1)S(1)}, bf16[512,640]{1,0:T(8,128)(2,1)S(1)}, u32[]{:S(2)}, u32[]{:S(2)}) collective-permute-start(bf16[512,640]{1,0:T(8,128)(2,1)S(1)} %get-tuple-element.36), channel_id=1, source_target_pairs={{0,6},{1,7},{2,0},{3,1},{4,2},{5,3},{6,4},{7,5},{8,14},{9,15},{10,... | collective-permute-start | bytes 1966088 | tf_op jit(solution)/shard_map/ppermute | solution.py:498
  120.9 22.3 %slice-start.2 = ((s8[5242880]{0:T(1024)(128)(4,1)}), s8[4194304]{0:T(1024)(128)(4,1)S(1)}, s32[]{:S(2)}) async-start(s8[5242880]{0:T(1024)(128)(4,1)} %bitcast.32), calls=%async_computation.4 | async-start | bytes 8388608
  120.9 24.4 %slice-start = ((s8[6553600]{0:T(1024)(128)(4,1)}), s8[4194304]{0:T(1024)(128)(4,1)S(1)}, s32[]{:S(2)}) async-start(s8[6553600]{0:T(1024)(128)(4,1)} %bitcast.28), calls=%async_computation.2 | async-start | bytes 8388608
  123.9 26.5 %collective-permute-start.17 = (bf16[512,640]{1,0:T(8,128)(2,1)S(1)}, bf16[512,640]{1,0:T(8,128)(2,1)S(1)}, u32[]{:S(2)}, u32[]{:S(2)}) collective-permute-start(bf16[512,640]{1,0:T(8,128)(2,1)S(1)} %get-tuple-element.38), channel_id=1, source_target_pairs={{0,2},{1,3},{2,4},{3,5},{4,6},{5,7},{6,0},{7,1},{8,10},{9,11},{10,... | collective-permute-start | bytes 1966088 | tf_op jit(solution)/shard_map/ppermute | solution.py:500
  125.5 17.6 %slice-start.3 = ((s8[5242880]{0:T(1024)(128)(4,1)}), s8[1048576]{0:T(1024)(128)(4,1)S(1)}, s32[]{:S(2)}) async-start(s8[5242880]{0:T(1024)(128)(4,1)} %bitcast.32), calls=%async_computation.5 | async-start | bytes 2097152
  125.5 17.6 %copy-start.4 = (bf16[128,5120]{1,0:T(8,128)(2,1)S(1)}, bf16[128,5120]{1,0:T(8,128)(2,1)}, u32[]{:S(2)}) copy-start(bf16[128,5120]{1,0:T(8,128)(2,1)} %p_ref.5) | copy-start | bytes 3932164
  125.5 19.8 %slice-start.1 = ((s8[6553600]{0:T(1024)(128)(4,1)}), s8[2359296]{0:T(1024)(128)(4,1)S(1)}, s32[]{:S(2)}) async-start(s8[6553600]{0:T(1024)(128)(4,1)} %bitcast.28), calls=%async_computation.3 | async-start | bytes 4718592
  125.5 26.5 %collective-permute-start.18 = (bf16[512,640]{1,0:T(8,128)(2,1)S(1)}, bf16[512,640]{1,0:T(8,128)(2,1)S(1)}, u32[]{:S(2)}, u32[]{:S(2)}) collective-permute-start(bf16[512,640]{1,0:T(8,128)(2,1)S(1)} %get-tuple-element.39), channel_id=1, source_target_pairs={{0,6},{1,7},{2,0},{3,1},{4,2},{5,3},{6,4},{7,5},{8,14},{9,15},{10,... | collective-permute-start | bytes 1966088 | tf_op jit(solution)/shard_map/ppermute | solution.py:501
  141.0 22.6 %collective-permute-start.16 = (bf16[512,640]{1,0:T(8,128)(2,1)S(1)}, bf16[512,640]{1,0:T(8,128)(2,1)S(1)}, u32[]{:S(2)}, u32[]{:S(2)}) collective-permute-start(bf16[512,640]{1,0:T(8,128)(2,1)S(1)} %get-tuple-element.37), channel_id=1, source_target_pairs={{0,2},{1,3},{2,4},{3,5},{4,6},{5,7},{6,0},{7,1},{8,10},{9,11},{10,... | collective-permute-start | bytes 1966088 | tf_op jit(solution)/shard_map/ppermute | solution.py:503
  142.3 22.5 %collective-permute-start.19 = (bf16[512,640]{1,0:T(8,128)(2,1)S(1)}, bf16[512,640]{1,0:T(8,128)(2,1)S(1)}, u32[]{:S(2)}, u32[]{:S(2)}) collective-permute-start(bf16[512,640]{1,0:T(8,128)(2,1)S(1)} %get-tuple-element.40), channel_id=1, source_target_pairs={{0,6},{1,7},{2,0},{3,1},{4,2},{5,3},{6,4},{7,5},{8,14},{9,15},{10,... | collective-permute-start | bytes 1966088 | tf_op jit(solution)/shard_map/ppermute | solution.py:504
  (4 other events, 15.9 us)
Sparse Core Ops, SparseCore 0:
  39.8 72.6 all-gather.2
